TPU v7x, 32 devices: a whole 2x2x4 slice. The times are simulated.
32 devices in a mesh: dp: 8 (over z, y), mp: 4 (over x, core).
Axes of the slice: x: 2, y: 2, z: 4, core: 2. Of those that a mesh axis runs over, the one named last changes fastest.
Arguments:
- tokens: bfloat16 [2, 16384, 768], P(None, ('dp', 'mp')), may hold values from -6 to 6
- cotangent: bfloat16 [2, 16384, 768], P(None, ('dp', 'mp')), may hold values from -6 to 6
- lengths: int32 [2, 16], P(None, 'dp'), may hold values from 341 to 1024, as said below
- w_query: bfloat16 [768, 768], P('dp', 'mp'), may hold values from -0.3125 to 0.3125
- w_key: bfloat16 [768, 768], P('dp', 'mp'), may hold values from -0.21875 to 0.21875
- w_value: bfloat16 [768, 768], P('dp', 'mp'), may hold values from -0.21875 to 0.21875
- w_out: bfloat16 [768, 768], P(('mp', 'dp')), may hold values from -0.875 to 0.875
- w_up: bfloat16 [768, 3072], P('dp', 'mp'), may hold values from -0.21875 to 0.21875
- w_down: bfloat16 [3072, 768], P(('mp', 'dp')), may hold values from -0.109375 to 0.109375
- b_query: float32 [768], P('mp'), may hold values from -3 to 3
- b_value: float32 [768], P('mp'), may hold values from -0.6 to 0.6
- b_up: float32 [3072], P('mp'), may hold values from -3 to 3
- b_out: float32 [768], replicated, may hold values from -0.6 to 0.6
- b_down: float32 [768], replicated, may hold values from -1.2 to 1.2
- norm1_gain: float32 [768], replicated, may hold values from 0.25 to 1.75
- norm1_shift: float32 [768], replicated, may hold values from -1.2 to 1.2
- norm2_gain: float32 [768], replicated, may hold values from 0.25 to 1.75
- norm2_shift: float32 [768], replicated, may hold values from -1.2 to 1.2
Outputs:
- output: bfloat16 [2, 16384, 768], P(None, ('dp', 'mp'))
- tokens_grad: float32 [2, 16384, 768], P(None, ('dp', 'mp'))
- w_query_grad: float32 [768, 768], P('dp', 'mp')
- w_key_grad: float32 [768, 768], P('dp', 'mp')
- w_value_grad: float32 [768, 768], P('dp', 'mp')
- w_out_grad: float32 [768, 768], P(('mp', 'dp'))
- w_up_grad: float32 [768, 3072], P('dp', 'mp')
- w_down_grad: float32 [3072, 768], P(('mp', 'dp'))
- b_query_grad: float32 [768], P(('mp', 'dp'))
- b_value_grad: float32 [768], P(('mp', 'dp'))
- b_up_grad: float32 [3072], P(('mp', 'dp'))
- b_out_grad: float32 [768], P(('dp', 'mp'))
- b_down_grad: float32 [768], P(('dp', 'mp'))
- norm1_gain_grad: float32 [768], P(('dp', 'mp'))
- norm1_shift_grad: float32 [768], P(('dp', 'mp'))
- norm2_gain_grad: float32 [768], P(('dp', 'mp'))
- norm2_shift_grad: float32 [768], P(('dp', 'mp'))
- rms_values: float32 [3], replicated
Inputs may be any that keep to these rules, and one draw needn't show every extreme that they name: The last sequence of every micro-batch has all 1024 positions valid; lengths tend to grow with the sequence's index.
All inputs are finite; a program needn't handle non-finite values.
Results may differ from a plain program's by a relative error of at most 0.019.
Values may be sent and summed in bfloat16 or wider, within the bound.
A program may use at most 192 MiB of HBM per device.

v0:
```python
import functools

import jax
import jax.numpy as jnp
from jax import lax
from jax.experimental import pallas as pl
from jax.experimental.pallas import tpu as pltpu
from jax.sharding import PartitionSpec as P

HD = 64
L = 1024
SEQ_MB = 2
MB = 2
GROUPS = 4
GH = 3
GC = GH * HD
PAD = 256

epsilon = 1e-05
masked_score = -1e30
exp2_scale = HD ** (-0.5) * 1.4426950408889634
score_scale = HD ** (-0.5)
BOTH = ("dp", "mp")
NT = (((1,), (1,)), ((), ()))


def product(left_side, right_side):
    return jnp.dot(left_side, right_side, preferred_element_type=jnp.float32)


def contract_rows(left_side, right_side):
    return lax.dot_general(
        left_side, right_side, (((0,), (0,)), ((), ())), preferred_element_type=jnp.float32
    )


def contract_cols(left_side, right_side):
    return lax.dot_general(left_side, right_side, NT, preferred_element_type=jnp.float32)


def layer_norm(values, norm_gain, norm_shift):
    center = values - jnp.mean(values, axis=-1, keepdims=True)
    spread = jnp.mean(center * center, axis=-1, keepdims=True)
    inverse = lax.rsqrt(spread + epsilon)
    scaled = center * inverse
    return (scaled * norm_gain + norm_shift, scaled, inverse)


def norm_back(upstream, scaled, inverse, norm_gain):
    gain_grad = jnp.sum(upstream * scaled, axis=0)
    shift_grad = jnp.sum(upstream, axis=0)
    through = upstream * norm_gain
    result = inverse * (
        through
        - jnp.mean(through, axis=-1, keepdims=True)
        - scaled * jnp.mean(through * scaled, axis=-1, keepdims=True)
    )
    return (result, gain_grad, shift_grad)


def head_keys(keys, bias, h, lane):
    kept = jnp.where((lane >= h * HD) & (lane < (h + 1) * HD), keys, jnp.zeros_like(keys))
    return jnp.where(lane == GC, bias, kept)


def attend_forward_kernel(bias_ref, qkv_ref, out_ref, lse_ref, turned):
    rows = qkv_ref.shape[1]
    chunk = 256
    lane = lax.broadcasted_iota(jnp.int32, (1, PAD), 1)
    keys = qkv_ref[0, :, PAD : 2 * PAD]
    values_t = qkv_ref[0, :, 2 * PAD :].T
    bias = bias_ref[...]
    for h in range(GH):
        own = head_keys(keys, bias, h, lane)
        own_values = values_t[h * HD : (h + 1) * HD, :]
        for at in range(0, rows, chunk):
            queries = qkv_ref[0, at : at + chunk, :PAD]
            scores = contract_cols(own, queries)
            top = jnp.max(scores, axis=0, keepdims=True) * exp2_scale
            raised = jnp.exp2(scores * exp2_scale - top)
            total = jnp.sum(raised, axis=0, keepdims=True)
            mixed = product(own_values, raised.astype(jnp.bfloat16))
            turned[h * HD : (h + 1) * HD, at : at + chunk] = mixed / total
            lse_ref[0, h : h + 1, at : at + chunk] = top + jnp.log2(total)
    turned[GC:, :] = jnp.zeros((PAD - GC, rows), jnp.float32)
    out_ref[0] = turned[...].T.astype(jnp.bfloat16)


def attend_forward(qkv, bias):
    rows = qkv.shape[1]
    return pl.pallas_call(
        attend_forward_kernel,
        grid=(GROUPS,),
        in_specs=[
            pl.BlockSpec((rows, 1), lambda g: (0, 0)),
            pl.BlockSpec((1, rows, 3 * PAD), lambda g: (g, 0, 0)),
        ],
        out_specs=[
            pl.BlockSpec((1, rows, PAD), lambda g: (g, 0, 0)),
            pl.BlockSpec((1, 8, rows), lambda g: (g, 0, 0)),
        ],
        out_shape=[
            jax.ShapeDtypeStruct((GROUPS, rows, PAD), jnp.bfloat16),
            jax.ShapeDtypeStruct((GROUPS, 8, rows), jnp.float32),
        ],
        scratch_shapes=[pltpu.VMEM((PAD, rows), jnp.float32)],
        cost_estimate=pl.CostEstimate(
            flops=45_000_000_000 // 3, bytes_accessed=10_000_000, transcendentals=12_000_000
        ),
    )(bias, qkv)


def attend_backward_kernel(
    bias_ref, qkv_ref, out_ref, lse_ref, grad_ref, joined_ref, sums_ref, probs, slopes, turned
):
    rows = qkv_ref.shape[1]
    chunk = 256
    lane = lax.broadcasted_iota(jnp.int32, (1, PAD), 1)
    keys = qkv_ref[0, :, PAD : 2 * PAD]
    keys_t = keys.T
    values = qkv_ref[0, :, 2 * PAD :]
    bias = bias_ref[...]
    crossed = (grad_ref[0].astype(jnp.float32) * out_ref[0].astype(jnp.float32)).T
    key_grad = jnp.zeros((rows, PAD), jnp.float32)
    value_grad = jnp.zeros((rows, PAD), jnp.float32)
    for h in range(GH):
        head = (lane >= h * HD) & (lane < (h + 1) * HD)
        own = head_keys(keys, bias, h, lane)
        own_values = jnp.where(head, values, jnp.zeros_like(values))
        delta = jnp.sum(crossed[h * HD : (h + 1) * HD, :], axis=0, keepdims=True)
        for at in range(0, rows, chunk):
            queries = qkv_ref[0, at : at + chunk, :PAD]
            grads = grad_ref[0, at : at + chunk, :]
            scores = contract_cols(own, queries)
            attn_probs = jnp.exp2(scores * exp2_scale - lse_ref[0, h : h + 1, at : at + chunk])
            prob_grad = contract_cols(own_values, grads)
            probs[:, at : at + chunk] = attn_probs.astype(jnp.bfloat16)
            slopes[:, at : at + chunk] = (
                attn_probs * (prob_grad - delta[:, at : at + chunk])
            ).astype(jnp.bfloat16)
        own_grads = jnp.where(head, grad_ref[0], jnp.zeros((), jnp.bfloat16))
        own_queries = jnp.where(head, qkv_ref[0, :, :PAD], jnp.zeros((), jnp.bfloat16))
        value_grad = value_grad + product(probs[...], own_grads)
        key_grad = key_grad + product(slopes[...], own_queries)
        turned[h * HD : (h + 1) * HD, :] = product(
            keys_t[h * HD : (h + 1) * HD, :], slopes[...]
        )
    turned[GC:, :] = jnp.zeros((PAD - GC, rows), jnp.float32)
    query_grad = turned[...].T * score_scale
    joined_ref[0, :, :PAD] = query_grad.astype(jnp.bfloat16)
    joined_ref[0, :, PAD : 2 * PAD] = (key_grad * score_scale).astype(jnp.bfloat16)
    joined_ref[0, :, 2 * PAD :] = value_grad.astype(jnp.bfloat16)
    sums_ref[0, 0:1, :] = jnp.sum(query_grad, axis=0, keepdims=True)
    sums_ref[0, 1:2, :] = jnp.sum(value_grad, axis=0, keepdims=True)


def attend_backward(qkv, bias, heads_out, lse, heads_grad):
    rows = qkv.shape[1]
    return pl.pallas_call(
        attend_backward_kernel,
        grid=(GROUPS,),
        in_specs=[
            pl.BlockSpec((rows, 1), lambda g: (0, 0)),
            pl.BlockSpec((1, rows, 3 * PAD), lambda g: (g, 0, 0)),
            pl.BlockSpec((1, rows, PAD), lambda g: (g, 0, 0)),
            pl.BlockSpec((1, 8, rows), lambda g: (g, 0, 0)),
            pl.BlockSpec((1, rows, PAD), lambda g: (g, 0, 0)),
        ],
        out_specs=[
            pl.BlockSpec((1, rows, 3 * PAD), lambda g: (g, 0, 0)),
            pl.BlockSpec((1, 8, PAD), lambda g: (g, 0, 0)),
        ],
        out_shape=[
            jax.ShapeDtypeStruct((GROUPS, rows, 3 * PAD), jnp.bfloat16),
            jax.ShapeDtypeStruct((GROUPS, 8, PAD), jnp.float32),
        ],
        scratch_shapes=[
            pltpu.VMEM((rows, rows), jnp.bfloat16),
            pltpu.VMEM((rows, rows), jnp.bfloat16),
            pltpu.VMEM((PAD, rows), jnp.float32),
        ],
        cost_estimate=pl.CostEstimate(
            flops=30_000_000_000, bytes_accessed=20_000_000, transcendentals=12_000_000
        ),
    )(bias, qkv, heads_out, lse, heads_grad)


def swap_with_partner(values):
    size = lax.axis_size("mp")
    return lax.ppermute(values, "mp", [(i, i ^ 1) for i in range(size)])


def pad_heads(values):
    return jnp.pad(values, [(0, 0)] * (values.ndim - 1) + [(0, PAD - values.shape[-1])])


MESH = pl.DeviceIdType.MESH


def positions():
    mp, dp = lax.axis_index("mp"), lax.axis_index("dp")
    return mp, lax.div(mp, 2), lax.rem(mp, 2), lax.div(dp, 2), lax.rem(dp, 2)


def at_place(x, c, z, y):
    return (2 * z + y, 2 * x + c)


def neighbours(nz):
    mp, x, c, z, y = positions()
    first = at_place(lax.rem(x + c, 2), c, z, lax.rem(y + 1 - c, 2))
    second = at_place(lax.rem(x + 1 - c, 2), c, z, lax.rem(y + c, 2))
    partner = at_place(x, 1 - c, z, y)
    along = [at_place(x, c, lax.rem(z + d, nz), y) for d in range(1, nz)]
    return first, second, partner, along


def meet(devices):
    barrier = pltpu.get_barrier_semaphore()
    for device in devices:
        pl.semaphore_signal(barrier, inc=1, device_id=device, device_id_type=MESH)
    pl.semaphore_wait(barrier, len(devices))


def regions(x, c, y):
    own = (x, y)
    first = (lax.rem(x + c, 2), lax.rem(y + 1 - c, 2))
    second = (lax.rem(x + 1 - c, 2), lax.rem(y + c, 2))
    third = (1 - x, 1 - y)
    return own, first, second, third


def gather_kernel(nz, parts, *refs):
    shards, fulls = refs[:parts], refs[parts : 2 * parts]
    own_sem, z_send, z_recv, send, recv = refs[2 * parts :]
    mp, x, c, z, y = positions()
    first, second, partner, along = neighbours(nz)
    meet([first, second, partner, *along])
    own, got1, got2, got3 = regions(x, c, y)
    other = regions(x, 1 - c, y)

    def remote(src, dst, s, r, device):
        return pltpu.make_async_remote_copy(
            src_ref=src, dst_ref=dst, send_sem=s, recv_sem=r, device_id=device, device_id_type=MESH
        )

    started = []
    locals_ = []
    spread = []
    for p in range(parts):
        keep = pltpu.make_async_copy(shards[p], fulls[p].at[x, c, z, y], own_sem.at[p])
        keep.start()
        locals_.append(keep)
        sends = [
            remote(shards[p], fulls[p].at[x, c, z, y], z_send.at[p, d], z_recv.at[p, d], along[d])
            for d in range(nz - 1)
        ]
        for copy in sends:
            copy.start()
        spread.append(sends)

    def block(p, core, place):
        return fulls[p].at[place[0], core, :, place[1]]

    def push(p, k, core, place, device):
        copy = remote(block(p, core, place), block(p, core, place), send.at[p, k], recv.at[p, k], device)
        copy.start()
        started.append(copy)
        return copy

    def arrived(p, k, core, place):
        here = block(p, core, place)
        remote(here, here, send.at[p, k], recv.at[p, k], first).wait_recv()

    for p in range(parts):
        locals_[p].wait()
        for copy in spread[p]:
            copy.wait_recv()
        push(p, 0, c, own, first)
        push(p, 1, c, own, second)
        push(p, 3, c, own, partner)
    for p in range(parts):
        arrived(p, 0, c, got1)
        push(p, 2, c, got1, second)
        push(p, 4, c, got1, partner)
    for p in range(parts):
        arrived(p, 1, c, got2)
        push(p, 5, c, got2, partner)
        arrived(p, 2, c, got3)
        push(p, 6, c, got3, partner)
    for p in range(parts):
        for k in range(4):
            arrived(p, 3 + k, 1 - c, other[k])
    for sends in spread:
        for copy in sends:
            copy.wait_send()
    for copy in started:
        copy.wait_send()


def gather_all(shards):
    n_dp = lax.axis_size("dp")
    nz, parts = n_dp // 2, len(shards)
    return pl.pallas_call(
        functools.partial(gather_kernel, nz, parts),
        in_specs=[pl.BlockSpec(memory_space=pltpu.VMEM)] * parts,
        out_specs=[pl.BlockSpec(memory_space=pl.ANY)] * parts,
        out_shape=[jax.ShapeDtypeStruct((2, 2, nz, 2, *s.shape), s.dtype) for s in shards],
        scratch_shapes=[
            pltpu.SemaphoreType.DMA((parts,)),
            pltpu.SemaphoreType.DMA((parts, nz - 1)),
            pltpu.SemaphoreType.DMA((parts, nz - 1)),
            pltpu.SemaphoreType.DMA((parts, 7)),
            pltpu.SemaphoreType.DMA((parts, 7)),
        ],
        compiler_params=pltpu.CompilerParams(collective_id=0, has_side_effects=True),
    )(*shards)


def scatter_kernel(nz, parts, side, *refs):
    partials, results = refs[:parts], refs[parts : 2 * parts]
    at = 2 * parts
    sums, heard1, heard2, heard3, heard4 = (
        refs[at + i * parts : at + (i + 1) * parts] for i in range(5)
    )
    own_sem, send, recv, z_send, z_recv = refs[at + 5 * parts :]
    mp, x, c, z, y = positions()
    first, second, partner, along = neighbours(nz)
    meet([first, second, partner, *along])
    own, got1, got2, got3 = regions(x, c, y)
    started = []

    def remote(src, dst, s, r, device):
        copy = pltpu.make_async_remote_copy(
            src_ref=src, dst_ref=dst, send_sem=s, recv_sem=r, device_id=device, device_id_type=MESH
        )
        copy.start()
        started.append(copy)
        return copy

    def add(p, place, more):
        for i in range(nz):
            here = sums[p].at[place[0], i, place[1]]
            here[...] = (here[...].astype(jnp.float32) + more[i].astype(jnp.float32)).astype(here.dtype)

    def cut(p, k, core):
        if p not in side:
            return partials[p].at[k, core]
        size = partials[p].shape[3] // 4
        return partials[p].at[:, :, :, pl.ds(pl.multiple_of((2 * k + core) * size, size), size)]

    kept, core_copies = [], []
    for p in range(parts):
        copies = []
        for k in range(2):
            keep = pltpu.make_async_copy(cut(p, k, c), sums[p].at[k], own_sem.at[p, k])
            keep.start()
            copies.append(keep)
        kept.append(copies)
        core_copies.append(
            [
                remote(cut(p, k, 1 - c), heard1[p].at[k], send.at[p, k], recv.at[p, k], partner)
                for k in range(2)
            ]
        )
    second_copies = []
    for p in range(parts):
        for copy in kept[p]:
            copy.wait()
        for copy in core_copies[p]:
            copy.wait_recv()
        copies = []
        for k, place in enumerate((got2, got3)):
            add(p, place, heard1[p].at[place[0], :, place[1]])
            copies.append(
                remote(
                    sums[p].at[place[0], :, place[1]],
                    heard2[p].at[k],
                    send.at[p, 2 + k],
                    recv.at[p, 2 + k],
                    second,
                )
            )
        second_copies.append(copies)
        for place in (got1, own):
            add(p, place, heard1[p].at[place[0], :, place[1]])
    first_copies = []
    for p in range(parts):
        second_copies[p][1].wait_recv()
        add(p, got1, heard2[p].at[1])
        first_copies.append(
            remote(sums[p].at[got1[0], :, got1[1]], heard3[p], send.at[p, 4], recv.at[p, 4], first)
        )
        second_copies[p][0].wait_recv()
        add(p, own, heard2[p].at[0])
    last_copies = []
    for p in range(parts):
        first_copies[p].wait_recv()
        add(p, own, heard3[p])
        last_copies.append(
            [
                remote(
                    sums[p].at[x, lax.rem(z + d + 1, nz), y],
                    heard4[p].at[d],
                    z_send.at[p, d],
                    z_recv.at[p, d],
                    along[d],
                )
                for d in range(nz - 1)
            ]
        )
    for p in range(parts):
        for copy in last_copies[p]:
            copy.wait_recv()
        total = sums[p][x, z, y].astype(jnp.float32)
        for d in range(nz - 1):
            total = total + heard4[p][d].astype(jnp.float32)
        results[p][...] = total
    for copy in started:
        copy.wait_send()


def scatter_sums(partials, side=()):
    nz, parts = lax.axis_size("dp") // 2, len(partials)
    tails = [
        (p.shape[2], p.shape[3] // 4) if i in side else p.shape[4:] for i, p in enumerate(partials)
    ]
    kinds = [p.dtype for p in partials]
    return pl.pallas_call(
        functools.partial(scatter_kernel, nz, parts, side),
        in_specs=[pl.BlockSpec(memory_space=pl.ANY)] * parts,
        out_specs=[pl.BlockSpec(memory_space=pltpu.VMEM)] * parts,
        out_shape=[jax.ShapeDtypeStruct(t, jnp.float32) for t in tails],
        scratch_shapes=[
            *[pltpu.VMEM((2, nz, 2, *t), k) for t, k in zip(tails, kinds)],
            *[pltpu.VMEM((2, nz, 2, *t), k) for t, k in zip(tails, kinds)],
            *[pltpu.VMEM((2, nz, *t), k) for t, k in zip(tails, kinds)],
            *[pltpu.VMEM((nz, *t), k) for t, k in zip(tails, kinds)],
            *[pltpu.VMEM((nz - 1, *t), k) for t, k in zip(tails, kinds)],
            pltpu.SemaphoreType.DMA((parts, 2)),
            pltpu.SemaphoreType.DMA((parts, 5)),
            pltpu.SemaphoreType.DMA((parts, 5)),
            pltpu.SemaphoreType.DMA((parts, nz - 1)),
            pltpu.SemaphoreType.DMA((parts, nz - 1)),
        ],
        compiler_params=pltpu.CompilerParams(
            collective_id=1, has_side_effects=True, vmem_limit_bytes=60 * 1024 * 1024
        ),
    )(*partials)


def in_place_order(blocks):
    return blocks.reshape(2, 2, blocks.shape[1] // 2, 2, *blocks.shape[2:])


def body_any(
    tokens,
    cotangent,
    lengths,
    w_query,
    w_key,
    w_value,
    w_out,
    w_up,
    w_down,
    b_query,
    b_value,
    b_up,
    b_out,
    b_down,
    norm1_gain,
    norm1_shift,
    norm2_gain,
    norm2_shift,
):
    half_rows = tokens.shape[1]
    width = tokens.shape[2]
    n_dp, n_mp = lax.axis_size("dp"), lax.axis_size("mp")
    unit_cols = w_up.shape[1]
    mp_index = lax.axis_index("mp")
    half = lax.rem(mp_index, 2)
    seq = lax.div(mp_index, 2)

    def own_of(pair):
        return jnp.where(half == 0, pair[0], pair[1])

    def other_of(pair):
        return jnp.where(half == 0, pair[1], pair[0])

    rows_in = jnp.concatenate([own_of(tokens), swap_with_partner(other_of(tokens))], axis=0)
    rows_cot = jnp.concatenate([own_of(cotangent), swap_with_partner(other_of(cotangent))], axis=0)
    length = lax.dynamic_slice(lengths, (half, seq), (1, 1))[0, 0]
    place = jnp.arange(half_rows, dtype=jnp.int32)
    place = jnp.concatenate([place + half * half_rows, place + (1 - half) * half_rows])
    valid_row = (place < length)[:, None]
    bias = jnp.where(valid_row, 0.0, masked_score).astype(jnp.bfloat16)
    valid_row = valid_row.astype(jnp.float32)

    biases = jnp.pad(jnp.concatenate([b_query, b_value, b_up]), (0, 896)).reshape(16, 128)
    qkv_shard = jnp.concatenate([w_query, w_key, w_value], axis=1)
    gathered = gather_all([qkv_shard, w_out, w_up, w_down, biases])
    full_qkv, full_out, full_up, full_down, full_bias = (
        g.reshape(n_mp, n_dp, *g.shape[4:]) for g in gathered
    )
    full_qkv = full_qkv.reshape(n_mp, width, 3, GC)
    w_joined = pad_heads(full_qkv).reshape(n_mp, width, 3 * PAD)
    full_out = full_out.reshape(n_mp, GC, width)
    out_pad = jnp.pad(full_out, ((0, 0), (0, PAD - GC), (0, 0))).reshape(n_mp * PAD, width)
    full_up = full_up.reshape(n_mp, width, unit_cols).transpose(1, 0, 2).reshape(width, n_mp * unit_cols)
    full_down = full_down.reshape(n_mp * unit_cols, width)
    full_bias = full_bias[:, 0].reshape(n_mp, -1)
    bias_q, bias_v, bias_up = full_bias[:, :GC], full_bias[:, GC:2*GC], full_bias[:, 2*GC:2*GC+unit_cols]
    mark = jnp.zeros((n_mp, PAD - GC), jnp.float32).at[:, 0].set(1.0)
    joined_bias = jnp.concatenate(
        [bias_q, mark, jnp.zeros((n_mp, PAD), jnp.float32), pad_heads(bias_v)], axis=1
    )

    qkv = lax.dot_general(
        jnp.broadcast_to(rows_in[None], (n_mp, *rows_in.shape)),
        w_joined,
        (((2,), (1,)), ((0,), (0,))),
        preferred_element_type=jnp.float32,
    )
    qkv = (qkv + joined_bias[:, None, :]).astype(jnp.bfloat16)
    heads_out, lse = attend_forward(qkv, bias)
    heads_flat = heads_out.transpose(1, 0, 2).reshape(2 * half_rows, n_mp * PAD)
    attention = product(heads_flat, out_pad) + b_out
    first_norm, first_scaled, first_inverse = layer_norm(
        rows_in.astype(jnp.float32) + attention, norm1_gain, norm1_shift
    )
    first_low = first_norm.astype(jnp.bfloat16)
    preact = product(first_low, full_up) + bias_up.reshape(-1)
    cumulative = 0.5 * (1.0 + lax.erf(preact * 0.7071067811865476))
    active = (preact * cumulative).astype(jnp.bfloat16)
    slope = cumulative + preact * (jnp.exp(-0.5 * preact * preact) * 0.3989422804014327)
    ffn_out = product(active, full_down) + b_down
    stream = first_norm + ffn_out
    final_norm, final_scaled, final_inverse = layer_norm(stream, norm2_gain, norm2_shift)
    output = final_norm.astype(jnp.bfloat16)
    squares = jnp.stack(
        [
            jnp.sum(valid_row * stream * stream),
            jnp.sum(valid_row * attention * attention),
            jnp.sum(valid_row * ffn_out * ffn_out),
            jnp.sum(valid_row),
        ]
    )

    stream_grad, gain2_grad, shift2_grad = norm_back(
        rows_cot.astype(jnp.float32), final_scaled, final_inverse, norm2_gain
    )
    down_bias_grad = jnp.sum(stream_grad, axis=0)
    ffn_grad_low = stream_grad.astype(jnp.bfloat16)
    active_grad = contract_cols(ffn_grad_low, full_down)
    down_wgrad = contract_rows(active, ffn_grad_low)
    preact_grad = active_grad * slope
    up_bias_grad = jnp.sum(preact_grad, axis=0)
    preact_low = preact_grad.astype(jnp.bfloat16)
    up_wgrad = contract_rows(first_low, preact_low)
    first_grad = stream_grad + contract_cols(preact_low, full_up)
    attn_grad, gain1_grad, shift1_grad = norm_back(
        first_grad, first_scaled, first_inverse, norm1_gain
    )
    out_bias_grad = jnp.sum(attn_grad, axis=0)
    attn_grad_low = attn_grad.astype(jnp.bfloat16)
    out_wgrad = contract_rows(heads_flat, attn_grad_low)
    heads_grad = contract_cols(attn_grad_low, out_pad).astype(jnp.bfloat16)
    heads_grad = heads_grad.reshape(2 * half_rows, n_mp, PAD).transpose(1, 0, 2)
    joined, sums = attend_backward(qkv, bias, heads_out, lse, heads_grad)
    joined_wgrad = lax.dot_general(
        jnp.broadcast_to(rows_in[None], (n_mp, *rows_in.shape)),
        joined,
        (((1,), (1,)), ((0,), (0,))),
        preferred_element_type=jnp.float32,
    )
    tokens_grad = attn_grad + jnp.sum(
        lax.dot_general(
            joined, w_joined, (((2,), (2,)), ((0,), (0,))), preferred_element_type=jnp.float32
        ),
        axis=0,
    )

    low = jnp.bfloat16
    joined_blocks = (
        joined_wgrad.astype(low)
        .reshape(n_mp, n_dp, width // n_dp, 3, PAD)[..., :GC]
        .reshape(n_mp, n_dp, width // n_dp, 3 * GC)
    )
    out_blocks = (
        out_wgrad.astype(low)
        .reshape(n_mp, PAD, width)[:, :GC]
        .reshape(n_mp, n_dp, GC // n_dp, width)
    )
    up_blocks = up_wgrad.astype(low).reshape(n_dp, width // n_dp, n_mp, unit_cols).transpose(2, 0, 1, 3)
    down_blocks = down_wgrad.astype(low).reshape(n_mp, n_dp, unit_cols // n_dp, width)

    def by_mp(vector):
        return vector.reshape(n_mp, n_dp, -1)

    def by_dp(vector):
        return vector.reshape(n_dp, n_mp, -1).transpose(1, 0, 2)

    vectors = [by_mp(sums[:, 0, :GC]), by_mp(sums[:, 1, :GC]), by_mp(up_bias_grad)]
    vectors += [
        by_dp(v)
        for v in (out_bias_grad, down_bias_grad, gain1_grad, shift1_grad, gain2_grad, shift2_grad)
    ]
    vectors.append(jnp.broadcast_to(squares, (n_mp, n_dp, 4)))
    ends = [v.shape[-1] for v in vectors]
    vectors = jnp.concatenate(vectors, axis=-1)
    vectors = jnp.pad(vectors, ((0, 0), (0, 0), (0, 1024 - vectors.shape[-1])))
    vectors = vectors.reshape(n_mp, n_dp, 8, 128)
    own_down, own_up, own_out, own_joined, own_vector = scatter_sums(
        [
            in_place_order(b)
            for b in (down_blocks, up_blocks, out_blocks, joined_blocks, vectors)
        ]
    )
    own_vector = own_vector.reshape(-1)
    own_vectors, start = [], 0
    for size in ends:
        own_vectors.append(own_vector[start : start + size])
        start += size
    totals = own_vectors.pop()
    rms_values = jnp.sqrt(totals[:3] / (totals[3] * width))

    def back_home(rows):
        mine, sent = rows[:half_rows], swap_with_partner(rows[half_rows:])
        return jnp.where(half == 0, jnp.stack([mine, sent]), jnp.stack([sent, mine]))

    return (
        back_home(output),
        back_home(tokens_grad),
        own_joined[:, :GC],
        own_joined[:, GC : 2 * GC],
        own_joined[:, 2 * GC :],
        own_out,
        own_up,
        own_down,
        *own_vectors,
        rms_values,
    )


PARTS = 4


def remote_copy(src, dst, s, r, device):
    return pltpu.make_async_remote_copy(
        src_ref=src, dst_ref=dst, send_sem=s, recv_sem=r, device_id=device, device_id_type=MESH
    )


def forward_kernel(
    nz,
    lengths,
    tokens,
    cotangent,
    shard_q,
    shard_o,
    shard_u,
    shard_d,
    bias_shard,
    full_q,
    full_o,
    full_u,
    full_d,
    bias_full,
    rows_out,
    cot_out,
    w_out,
    qkv_out,
    heads_out,
    lse_out,
    rows,
    cots,
    w_got,
    w_pad,
    qkv,
    values_t,
    turned,
    heads,
    own_sem,
    z_send,
    z_recv,
    relay_send,
    send,
    recv,
    swap_send,
    swap_recv,
    bias_send,
    bias_recv,
    out_sem,
):
    shards = (shard_q, shard_o, shard_u, shard_d)
    fulls = (full_q, full_o, full_u, full_d)
    half_rows = tokens.shape[1]
    length = 2 * half_rows
    mp, x, c, z, y = positions()
    half = c
    seq = x
    first, second, partner, along = neighbours(nz)
    across = at_place(1 - x, c, z, y)
    slanted = at_place(1 - x, 1 - c, z, y)
    own, got1, got2, got3 = regions(x, c, y)
    other = regions(x, 1 - c, y)
    meet([first, second, partner, slanted, *along])

    def block(p, core, place, d):
        return fulls[p].at[place[0], core, lax.rem(z + nz - d, nz), place[1]]

    places = (own, own, got1, own, got1, got2, got3)
    targets = (first, second, second, partner, partner, partner, partner)
    landing = (got1, got2, got3, *other)
    cores = (c, c, c, 1 - c, 1 - c, 1 - c, 1 - c)

    def outgoing(p, k, d):
        here = block(p, c, places[k], d)
        return remote_copy(here, here, send.at[p, k, d], recv.at[p, k, d], targets[k])

    def incoming(p, k, d):
        here = block(p, cores[k], landing[k], d)
        return remote_copy(here, here, send.at[p, k, d], recv.at[p, k, d], targets[k])

    at_low = 1 - lax.div(z + nz - 1, nz)
    near, far = 1 + 2 * at_low, 3 - 2 * at_low

    def z_copy(p, d):
        return remote_copy(
            shards[p], fulls[p].at[x, c, z, y], z_send.at[p, d - 1], z_recv.at[p, d - 1], along[d - 1]
        )

    def z_each(p, act):
        act(z_copy(p, 2))
        pl.when(z != nz - 1)(lambda: act(z_copy(p, 1)))
        pl.when(z != 0)(lambda: act(z_copy(p, 3)))

    def z_start(p):
        z_each(p, lambda copy: copy.start())

    def z_relay(p, low):
        here = block(p, c, own, 2)
        d = 1 if low else 3
        return remote_copy(here, here, relay_send.at[p], z_recv.at[p, d - 1], at_place(x, c, z + d - 2, y))

    def spread(p, d):
        if not (isinstance(d, int) and d == 0):
            here = block(p, c, own, d)
            remote_copy(here, here, z_send.at[p, d - 1], z_recv.at[p, d - 1], first).wait_recv()
        if isinstance(d, int) and d == 2:
            pl.when(z == 1)(lambda: z_relay(p, True).start())
            pl.when(z == 2)(lambda: z_relay(p, False).start())
        for k in (0, 1, 3):
            outgoing(p, k, d).start()

    def forward1(p):
        for d in range(nz):
            incoming(p, 0, d).wait_recv()
            outgoing(p, 2, d).start()
            outgoing(p, 4, d).start()

    def forward2(p):
        for d in range(nz):
            incoming(p, 1, d).wait_recv()
            outgoing(p, 5, d).start()

    def forward3(p):
        for d in range(nz):
            incoming(p, 2, d).wait_recv()
            outgoing(p, 6, d).start()

    def take(p, k):
        for d in range(nz):
            incoming(p, k, d).wait_recv()

    keep = [
        pltpu.make_async_copy(shards[p], fulls[p].at[x, c, z, y], own_sem.at[p]) for p in range(PARTS)
    ]
    keep_rows = pltpu.make_async_copy(tokens.at[half], rows.at[pl.ds(0, half_rows)], own_sem.at[PARTS])
    keep_cots = pltpu.make_async_copy(cotangent.at[half], cots.at[pl.ds(0, half_rows)], own_sem.at[PARTS + 2])
    swap_rows = remote_copy(
        tokens.at[1 - half], rows.at[pl.ds(half_rows, half_rows)], swap_send.at[0], swap_recv.at[0], partner
    )
    swap_cot = remote_copy(
        cotangent.at[1 - half], cots.at[pl.ds(half_rows, half_rows)], swap_send.at[1], swap_recv.at[1], partner
    )
    bias_copies = [
        remote_copy(bias_shard, bias_full.at[mp], bias_send.at[k], bias_recv.at[k], device)
        for k, device in enumerate((partner, across, slanted))
    ]
    z_start(0)
    keep[0].start()
    for copy in bias_copies:
        copy.start()
    swap_rows.start()
    keep_rows.start()
    for p in range(1, PARTS):
        keep[p].start()
    keep[0].wait()
    spread(0, 0)
    for p in range(1, PARTS):
        z_start(p)
    w_pad[...] = jnp.zeros_like(w_pad)
    turned[...] = jnp.zeros_like(turned)
    bias_full[mp] = bias_shard[...]
    for d in (2, near, far):
        spread(0, d)
    for copy in keep[1:]:
        copy.wait()
    forward1(0)
    for p in range(1, PARTS):
        spread(p, 0)
    forward2(0)
    swap_cot.start()
    keep_cots.start()
    keep_rows.wait()
    swap_rows.wait_recv()
    rows_copy = pltpu.make_async_copy(rows, rows_out, out_sem.at[2])
    rows_copy.start()
    cots_copy = pltpu.make_async_copy(cots, cot_out, out_sem.at[4])
    for copy in bias_copies:
        copy.wait_recv()

    hooks = {
        0: [lambda: [spread(1, d) for d in (2, near, far)]],
        1: [lambda: forward3(0)],
        2: [lambda: [spread(2, d) for d in (2, near)]],
        3: [lambda: spread(2, far), lambda: forward1(1)],
        4: [lambda: forward2(1), lambda: forward3(1)],
        5: [lambda: [spread(3, d) for d in (2, near)]],
        6: [lambda: spread(3, far)],
        7: [lambda: forward1(2)],
        8: [lambda: forward2(2)],
        10: [lambda: forward1(3)],
        11: [lambda: forward2(3)],
    }
    seq_length = lengths[half, seq]
    row = lax.broadcasted_iota(jnp.int32, (length, 1), 0)
    place = jnp.where(row < half_rows, row + half * half_rows, row - half * half_rows)
    bias = jnp.where(place < seq_length, 0.0, masked_score).astype(jnp.bfloat16)
    lane = lax.broadcasted_iota(jnp.int32, (1, PAD), 1)
    chunk = 256

    def heads_copy(gx, gc):
        columns = pl.ds(pl.multiple_of((2 * gx + gc) * PAD, PAD), PAD)
        return pltpu.make_async_copy(heads, heads_out.at[:, columns], out_sem.at[0])

    def qkv_copy(gx, gc):
        return pltpu.make_async_copy(qkv, qkv_out.at[2 * gx + gc], out_sem.at[1])

    def w_copy(gx, gc):
        return pltpu.make_async_copy(w_pad, w_out.at[2 * gx + gc], out_sem.at[3])

    def group_step(r, carry):
        gx, gc = lax.rem(x + lax.div(r, 2), 2), lax.rem(c + lax.rem(r, 2), 2)
        group = 2 * gx + gc

        @pl.when(r == 1)
        def _():
            for d in range(nz):
                incoming(0, 3, d).wait_recv()
            for d in range(nz):
                here = block(0, 1 - c, own, d)
                remote_copy(here, here, send.at[0, 5 - c, d], recv.at[0, 5 - c, d], first).wait_recv()

        @pl.when(r == 3)
        def _():
            for d in range(nz):
                here = block(0, 1 - c, own, d)
                remote_copy(here, here, send.at[0, 4 + c, d], recv.at[0, 4 + c, d], first).wait_recv()
            take(0, 6)

        load = pltpu.make_async_copy(full_q.at[gx, gc], w_got, own_sem.at[PARTS + 1])
        load.start()
        load.wait()

        @pl.when(r > 0)
        def _():
            qkv_copy(gx, gc).wait()
            w_copy(gx, gc).wait()

        w_flat = w_got[...].reshape(-1, 3 * GC)
        for k in range(3):
            w_pad[:, k * PAD : k * PAD + GC] = w_flat[:, k * GC : (k + 1) * GC]
        w_copy(gx, gc).start()
        joined_bias = bias_full[group, 0:1, :]
        for at in range(0, length, 512):
            qkv[at : at + 512, :] = (product(rows[at : at + 512, :], w_pad[...]) + joined_bias).astype(
                jnp.bfloat16
            )
        qkv_copy(gx, gc).start()
        values_t[...] = qkv[:, 2 * PAD :].T

        def head_step(h, carry):
            for k, todo in hooks.items():
                if todo:

                    @pl.when(r * GH + h == k)
                    def _():
                        for task in todo:
                            task()

            start = h * HD
            keys = qkv[:, PAD : 2 * PAD]
            kept = jnp.where((lane >= start) & (lane < start + HD), keys, jnp.zeros_like(keys))
            own_keys = jnp.where(lane == GC, bias, kept)
            own_values = values_t[pl.ds(pl.multiple_of(start, HD), HD), :]
            for at in range(0, length, chunk):
                scores = contract_cols(own_keys, qkv[at : at + chunk, :PAD])
                top = jnp.max(scores, axis=0, keepdims=True) * exp2_scale
                raised = jnp.exp2(scores * exp2_scale - top)
                total = jnp.sum(raised, axis=0, keepdims=True)
                mixed = product(own_values, raised.astype(jnp.bfloat16))
                turned[pl.ds(pl.multiple_of(start, HD), HD), at : at + chunk] = mixed / total
                lse_out[group, pl.ds(h, 1), at : at + chunk] = top + jnp.log2(total)
            return carry

        lax.fori_loop(0, GH, head_step, 0)

        @pl.when(r > 0)
        def _():
            heads_copy(gx, gc).wait()

        heads[...] = turned[...].T.astype(jnp.bfloat16)
        heads_copy(gx, gc).start()
        return carry

    lax.fori_loop(0, GROUPS, group_step, 0)
    keep_cots.wait()
    swap_cot.wait_recv()
    cots_copy.start()
    forward3(2)
    forward3(3)
    for p in range(1, PARTS):
        for k in range(3, 7):
            take(p, k)
    heads_copy(x, c).wait()
    qkv_copy(x, c).wait()
    w_copy(x, c).wait()
    rows_copy.wait()
    cots_copy.wait()
    swap_cot.wait_send()
    swap_rows.wait_send()
    for copy in bias_copies:
        copy.wait_send()
    for p in range(PARTS):
        z_each(p, lambda copy: copy.wait_send())
        pl.when(z == 1)(lambda: z_relay(p, True).wait_send())
        pl.when(z == 2)(lambda: z_relay(p, False).wait_send())
        for k in range(7):
            for d in range(nz):
                outgoing(p, k, d).wait_send()


def forward_attention(lengths, tokens, cotangent, shards, bias_shard):
    nz = lax.axis_size("dp") // 2
    half_rows, width = tokens.shape[1:]
    rows = 2 * half_rows
    low = jnp.bfloat16
    anywhere, vmem = pl.BlockSpec(memory_space=pl.ANY), pl.BlockSpec(memory_space=pltpu.VMEM)
    dma = pltpu.SemaphoreType.DMA
    return pl.pallas_call(
        functools.partial(forward_kernel, nz),
        in_specs=[pl.BlockSpec(memory_space=pltpu.SMEM), anywhere, anywhere, *[vmem] * 5],
        out_specs=[*[anywhere] * PARTS, vmem, *[anywhere] * 5, vmem],
        out_shape=[
            *[jax.ShapeDtypeStruct((2, 2, nz, 2, *s.shape), s.dtype) for s in shards],
            jax.ShapeDtypeStruct((GROUPS, *bias_shard.shape), jnp.float32),
            jax.ShapeDtypeStruct((rows, width), low),
            jax.ShapeDtypeStruct((rows, width), low),
            jax.ShapeDtypeStruct((GROUPS, width, 3 * PAD), low),
            jax.ShapeDtypeStruct((GROUPS, rows, 3 * PAD), low),
            jax.ShapeDtypeStruct((rows, GROUPS * PAD), low),
            jax.ShapeDtypeStruct((GROUPS, 8, rows), jnp.float32),
        ],
        scratch_shapes=[
            pltpu.VMEM((rows, width), low),
            pltpu.VMEM((rows, width), low),
            pltpu.VMEM((nz, 2, *shards[0].shape), low),
            pltpu.VMEM((width, 3 * PAD), low),
            pltpu.VMEM((rows, 3 * PAD), low),
            pltpu.VMEM((PAD, rows), low),
            pltpu.VMEM((PAD, rows), jnp.float32),
            pltpu.VMEM((rows, PAD), low),
            dma((PARTS + 3,)),
            dma((PARTS, nz - 1)),
            dma((PARTS, nz - 1)),
            dma((PARTS,)),
            dma((PARTS, 7, nz)),
            dma((PARTS, 7, nz)),
            dma((2,)),
            dma((2,)),
            dma((3,)),
            dma((3,)),
            dma((5,)),
        ],
        compiler_params=pltpu.CompilerParams(
            collective_id=2, has_side_effects=True, vmem_limit_bytes=60 * 1024 * 1024
        ),
    )(lengths, tokens, cotangent, *shards, bias_shard)


def place_of(info_ref, row, half_rows):
    half = info_ref[1]
    return jnp.where(row < half_rows, row + half * half_rows, row - half * half_rows)


def dense_kernel(
    info_ref,
    heads_ref,
    rows_ref,
    cot_ref,
    out_w,
    up_w,
    down_w,
    vec_ref,
    bias_ref,
    output_ref,
    first_ref,
    active_ref,
    ffn_low_ref,
    preact_low_ref,
    attn_ref,
    attn_low_ref,
    heads_grad_ref,
    sums_ref,
    slope,
):
    t = pl.program_id(0)
    low = jnp.bfloat16
    tile, width = rows_ref.shape
    units = up_w.shape[2]
    b_out, b_down, gain1, shift1, gain2, shift2 = (vec_ref[k : k + 1, :] for k in range(6))

    @pl.when(t == 0)
    def _():
        sums_ref[...] = jnp.zeros_like(sums_ref)

    def count(k, values):
        sums_ref[k : k + 1, :] += jnp.sum(values, axis=0, keepdims=True)

    attention = product(heads_ref[...], out_w[...]) + b_out
    first_norm, first_scaled, first_inverse = layer_norm(
        rows_ref[...].astype(jnp.float32) + attention, gain1, shift1
    )
    first_low = first_norm.astype(low)
    first_ref[...] = first_low
    ffn_out = jnp.broadcast_to(b_down, (tile, width))
    for g in range(GROUPS):
        preact = product(first_low, up_w[g]) + bias_ref[g, 1:2, :]
        cumulative = 0.5 * (1.0 + lax.erf(preact * 0.7071067811865476))
        active = (preact * cumulative).astype(low)
        active_ref[:, g * units : (g + 1) * units] = active
        slope[:, g * units : (g + 1) * units] = cumulative + preact * (
            jnp.exp(-0.5 * preact * preact) * 0.3989422804014327
        )
        ffn_out = ffn_out + product(active, down_w[g])
    stream = first_norm + ffn_out
    row = lax.broadcasted_iota(jnp.int32, (tile, 1), 0) + t * tile
    valid = (place_of(info_ref, row, pl.num_programs(0) * tile // 2) < info_ref[0]).astype(jnp.float32)
    count(6, valid * stream * stream)
    count(7, valid * attention * attention)
    count(8, valid * ffn_out * ffn_out)
    count(9, jnp.broadcast_to(valid, (tile, width)))
    final_norm, final_scaled, final_inverse = layer_norm(stream, gain2, shift2)
    output_ref[...] = final_norm.astype(low)

    def norm_step(k, upstream, scaled, inverse, gain):
        count(k, upstream * scaled)
        count(k + 1, upstream)
        through = upstream * gain
        return inverse * (
            through
            - jnp.mean(through, axis=-1, keepdims=True)
            - scaled * jnp.mean(through * scaled, axis=-1, keepdims=True)
        )

    stream_grad = norm_step(4, cot_ref[...].astype(jnp.float32), final_scaled, final_inverse, gain2)
    count(1, stream_grad)
    ffn_grad_low = stream_grad.astype(low)
    ffn_low_ref[...] = ffn_grad_low
    first_grad = stream_grad
    for g in range(GROUPS):
        preact_grad = contract_cols(ffn_grad_low, down_w[g]) * slope[:, g * units : (g + 1) * units]
        count(12 + g, preact_grad)
        preact_low = preact_grad.astype(low)
        preact_low_ref[:, g * units : (g + 1) * units] = preact_low
        first_grad = first_grad + contract_cols(preact_low, up_w[g])
    attn_grad = norm_step(2, first_grad, first_scaled, first_inverse, gain1)
    count(0, attn_grad)
    attn_ref[...] = attn_grad
    attn_grad_low = attn_grad.astype(low)
    attn_low_ref[...] = attn_grad_low
    heads_grad_ref[...] = contract_cols(attn_grad_low, out_w[...]).astype(low)


def dense(info, heads, rows, cots, out_w, up_w, down_w, vecs, biases):
    count, width = rows.shape
    tile = 256
    units = up_w.shape[2]
    low = jnp.bfloat16

    def whole(shape):
        return pl.BlockSpec(shape, lambda t: (0,) * len(shape))

    def tiled(columns):
        return pl.BlockSpec((tile, columns), lambda t: (t, 0))

    outs = [
        (width, low),
        (width, low),
        (GROUPS * units, low),
        (width, low),
        (GROUPS * units, low),
        (width, jnp.float32),
        (width, low),
        (GROUPS * PAD, low),
    ]
    return pl.pallas_call(
        dense_kernel,
        grid=(count // tile,),
        in_specs=[
            pl.BlockSpec(memory_space=pltpu.SMEM),
            tiled(GROUPS * PAD),
            tiled(width),
            tiled(width),
            whole(out_w.shape),
            whole(up_w.shape),
            whole(down_w.shape),
            whole(vecs.shape),
            whole(biases.shape),
        ],
        out_specs=[*[tiled(columns) for columns, _ in outs], whole((16, width))],
        out_shape=[
            *[jax.ShapeDtypeStruct((count, columns), kind) for columns, kind in outs],
            jax.ShapeDtypeStruct((16, width), jnp.float32),
        ],
        scratch_shapes=[pltpu.VMEM((tile, GROUPS * units), jnp.float32)],
        cost_estimate=pl.CostEstimate(
            flops=22_600_000_000, bytes_accessed=40_000_000, transcendentals=7_000_000
        ),
    )(info, heads, rows, cots, out_w, up_w, down_w, vecs, biases)


BIG = 4


def backward_kernel(
    nz,
    info,
    lse_ref,
    dense_sums,
    rows_in,
    w_joined,
    attn_grad,
    qkv,
    heads,
    heads_grad,
    active,
    ffn_low,
    first_low,
    preact_low,
    attn_low,
    down_out,
    up_out,
    out_out,
    query_out,
    key_out,
    value_out,
    dense_total,
    head_total,
    tokens_out,
    *refs,
):
    parts, heard1, heard2, heard3, heard4 = (refs[BIG * i : BIG * (i + 1)] for i in range(5))
    (
        dense_kept,
        head_kept,
        dense_heard,
        head_heard,
        acc,
        slots,
        right,
        left_t,
        joined,
        heads_in,
        grad_in,
        w_in,
        tokens,
        probs,
        slopes,
        turned,
        crossed,
        keys_t,
        key_acc,
        value_acc,
        send,
        recv,
        z_send,
        z_recv,
        v_send,
        v_recv,
        swap_sem,
        load_sem,
        slot_sem,
        heads_sem,
        grad_sem,
    ) = refs[5 * BIG :]
    low = jnp.bfloat16
    rows, width = tokens.shape
    half_rows = rows // 2
    chunk, span = 256, 384
    mp, x, c, z, y = positions()
    first, second, partner, along = neighbours(nz)
    own, got1, got2, got3 = regions(x, c, y)

    def group_of(r):
        return lax.rem(x + 1 + lax.rem(r, 2), 2), lax.rem(c + 1 + lax.div(r, 2), 2)

    def index_of(r):
        gx, gc = group_of(r)
        return 2 * gx + gc

    def columns(r, size):
        return pl.ds(pl.multiple_of(index_of(r) * size, size), size)

    def load(src, dst, k):
        return pltpu.make_async_copy(src, dst, load_sem.at[k])

    def slot_load(src, s):
        return pltpu.make_async_copy(src, slots.at[s], slot_sem.at[s])

    def active_load(r):
        return slot_load(active.at[:, columns(r, width)], lax.rem(r, 2))

    def preact_load(r):
        return slot_load(preact_low.at[:, columns(r, width)], lax.rem(r, 2))

    def qkv_load(r):
        return slot_load(qkv.at[index_of(r)], lax.rem(r, 2))

    def heads_load(r):
        s = lax.rem(r, 2)
        return pltpu.make_async_copy(heads.at[:, columns(r, PAD)], heads_in.at[s], heads_sem.at[s])

    def grad_load(r):
        s = lax.rem(r, 2)
        return pltpu.make_async_copy(heads_grad.at[:, columns(r, PAD)], grad_in.at[s], grad_sem.at[s])

    def w_load(r):
        return load(w_joined.at[index_of(r)], w_in, 3)

    ffn_load, attn_low_load = load(ffn_low, right, 0), load(attn_low, right, 0)
    first_load, rows_load = load(first_low, joined, 1), load(rows_in, joined, 1)
    tokens_load = load(attn_grad, tokens, 2)

    def core_copy(p, r):
        gx, gc = group_of(r)
        return remote_copy(parts[p].at[gx, gc], heard1[p].at[r], send.at[p, r], recv.at[p, r], partner)

    def second_copy(p, k):
        place = (got2, got3)[k]
        return remote_copy(
            parts[p].at[place[0], c, :, place[1]], heard2[p].at[k], send.at[p, 2 + k], recv.at[p, 2 + k], second
        )

    def first_copy(p):
        return remote_copy(
            parts[p].at[got1[0], c, :, got1[1]], heard3[p], send.at[p, 4], recv.at[p, 4], first
        )

    def z_copy(p, d):
        return remote_copy(
            parts[p].at[x, c, lax.rem(z + d + 1, nz), y],
            heard4[p].at[d],
            z_send.at[p, d],
            z_recv.at[p, d],
            along[d],
        )

    def add(p, place, more):
        for i in range(nz):
            here = parts[p].at[place[0], c, i, place[1]]
            here[...] = (here[...].astype(jnp.float32) + more[i].astype(jnp.float32)).astype(low)

    def take_second(p, k):
        second_copy(p, k).wait_recv()
        add(p, got1 if k else own, heard2[p].at[k])

    def pass_first(p):
        take_second(p, 1)
        first_copy(p).start()

    def take_first(p):
        first_copy(p).wait_recv()
        add(p, own, heard3[p])
        for d in range(nz - 1):
            z_copy(p, d).start()

    def take_z(p):
        total = parts[p][x, c, z, y].astype(jnp.float32)
        for d in range(nz - 1):
            z_copy(p, d).wait_recv()
            total = total + heard4[p][d].astype(jnp.float32)
        if p < BIG - 1:
            (down_out, up_out, out_out)[p][...] = total
        else:
            for k, result in enumerate((query_out, key_out, value_out)):
                result[...] = total[:, k * GC : (k + 1) * GC]

    kept, heard_sums = (dense_kept, head_kept), (dense_heard, head_heard)

    def sums_copy(v, k):
        device = (first, second)[k - 1] if 0 < k < 3 else along[k - 3] if k else partner
        return remote_copy(
            kept[v].at[min(k, 3)], heard_sums[v].at[k], v_send.at[v, k], v_recv.at[v, k], device
        )

    def sums_step(v, k):
        sums_copy(v, k).wait_recv()
        kept[v][k + 1] = kept[v][k] + heard_sums[v][k]
        for later in (k + 1,) if k < 2 else range(3, nz + 2):
            sums_copy(v, later).start()

    def sums_last(v):
        total = kept[v][3]
        for k in range(3, nz + 2):
            sums_copy(v, k).wait_recv()
            total = total + heard_sums[v][k]
        (dense_total, head_total)[v][...] = total

    def finish(p, r):
        gx, gc = group_of(r)
        deep, wide = parts[p].shape[4:]
        pieces = [(0, 0, wide)] if p < BIG - 1 else [(k * GC, k * PAD, GC) for k in range(3)]

        def put(more):
            for i in range(nz):
                for at, source, size in pieces:
                    value = acc[2 * deep * i : 2 * deep * (i + 1), source : source + size].reshape(2, deep, size)
                    if more is not None:
                        value = value + more[i, :, :, at : at + size].astype(jnp.float32)
                    parts[p][gx, gc, i, :, :, at : at + size] = value.astype(low)

        @pl.when(r < 2)
        def _():
            put(None)
            core_copy(p, r).start()

        @pl.when(r >= 2)
        def _():
            core_copy(p, r - 2).wait_recv()
            put(heard1[p].at[r - 2])

        @pl.when(r == 2)
        def _():
            second_copy(p, 1).start()
            pl.when(c == 0)(lambda: second_copy(p, 0).start())

        @pl.when(r == 3)
        def _():
            pl.when(c == 1)(lambda: second_copy(p, 0).start())

    ffn_load.start()
    active_load(0).start()
    heads_load(0).start()
    first_load.start()
    w_load(0).start()
    tokens_load.start()
    meet([first, second, partner, *along])
    dense_kept[0] = dense_sums[...]
    ffn_load.wait()

    def down_step(r, carry):
        active_load(r).wait()
        pl.when(r < 3)(lambda: active_load(r + 1).start())
        pl.when(r == 3)(lambda: preact_load(0).start())
        s = lax.rem(r, 2)
        for at in range(0, width, span):
            acc[at : at + span, :] = product(slots[s, :, at : at + span].T, right[...])
        finish(0, r)
        return carry

    lax.fori_loop(0, GROUPS, down_step, 0)
    sums_copy(0, 0).start()
    attn_low_load.start()
    first_load.wait()
    left_t[...] = joined[...].T
    rows_load.start()

    def up_step(r, carry):
        preact_load(r).wait()
        pl.when(r < 3)(lambda: preact_load(r + 1).start())
        pl.when(r == 3)(lambda: qkv_load(0).start())
        s = lax.rem(r, 2)
        for at in range(0, width, span):
            acc[at : at + span, :] = product(left_t[at : at + span, :], slots[s])
        finish(1, r)
        return carry

    lax.fori_loop(0, GROUPS, up_step, 0)
    sums_step(0, 0)
    attn_low_load.wait()

    def out_step(r, carry):
        heads_load(r).wait()
        heads_load(lax.rem(r + 1, GROUPS)).start()
        acc[:PAD, :] = product(heads_in[lax.rem(r, 2)].T, right[...])
        finish(2, r)
        return carry

    lax.fori_loop(0, GROUPS, out_step, 0)
    grad_load(0).start()
    rows_load.wait()
    left_t[...] = joined[...].T
    tokens_load.wait()

    hooks = {
        0: lambda: sums_step(0, 1),
        1: lambda: (pass_first(0), take_second(0, 0)),
        2: lambda: sums_step(0, 2),
        4: lambda: take_first(0),
        5: lambda: (pass_first(1), take_second(1, 0)),
        6: lambda: (pass_first(2), take_second(2, 0)),
        8: lambda: take_first(1),
        9: lambda: (take_first(2), sums_last(0)),
        10: lambda: take_z(0),
        11: lambda: pl.when(c == 1)(lambda: pass_first(3)),
    }
    row = lax.broadcasted_iota(jnp.int32, (rows, 1), 0)
    bias = jnp.where(place_of(info, row, half_rows) < info[0], 0.0, masked_score).astype(low)
    lane = lax.broadcasted_iota(jnp.int32, (1, PAD), 1)
    turned[...] = jnp.zeros_like(turned)

    def group_step(r, carry):
        s = lax.rem(r, 2)
        group = index_of(r)
        for copy in (qkv_load, heads_load, grad_load):
            copy(r).wait()

        @pl.when(r < 3)
        def _():
            for copy in (qkv_load, heads_load, grad_load):
                copy(r + 1).start()

        crossed[...] = (grad_in[s].astype(jnp.float32) * heads_in[s].astype(jnp.float32)).T
        keys_t[...] = slots[s, :, PAD : 2 * PAD].T
        key_acc[...] = jnp.zeros_like(key_acc)
        value_acc[...] = jnp.zeros_like(value_acc)

        def head_step(h, carry):
            for k, todo in hooks.items():
                pl.when(r * GH + h == k)(todo_of(todo))
            start = pl.multiple_of(h * HD, HD)
            head = (lane >= start) & (lane < start + HD)
            keys = slots[s, :, PAD : 2 * PAD]
            own_keys = jnp.where(lane == GC, bias, jnp.where(head, keys, jnp.zeros_like(keys)))
            own_values = jnp.where(head, slots[s, :, 2 * PAD :], jnp.zeros((), low))
            delta = jnp.sum(crossed[pl.ds(start, HD), :], axis=0, keepdims=True)
            for at in range(0, rows, chunk):
                scores = contract_cols(own_keys, slots[s, at : at + chunk, :PAD])
                attn_probs = jnp.exp2(scores * exp2_scale - lse_ref[group, pl.ds(h, 1), at : at + chunk])
                prob_grad = contract_cols(own_values, grad_in[s, at : at + chunk, :])
                probs[:, at : at + chunk] = attn_probs.astype(low)
                slopes[:, at : at + chunk] = (
                    attn_probs * (prob_grad - delta[:, at : at + chunk])
                ).astype(low)
            own_grads = jnp.where(head, grad_in[s], jnp.zeros((), low))
            own_queries = jnp.where(head, slots[s, :, :PAD], jnp.zeros((), low))
            value_acc[...] += product(probs[...], own_grads)
            key_acc[...] += product(slopes[...], own_queries)
            turned[pl.ds(start, HD), :] = product(keys_t[pl.ds(start, HD), :], slopes[...])
            return carry

        lax.fori_loop(0, GH, head_step, 0)
        query_grad = turned[...].T * score_scale
        joined[:, :PAD] = query_grad.astype(low)
        joined[:, PAD : 2 * PAD] = (key_acc[...] * score_scale).astype(low)
        joined[:, 2 * PAD :] = value_acc[...].astype(low)
        head_kept[0, pl.ds(group, 1), :] = jnp.sum(query_grad, axis=0, keepdims=True)
        head_kept[0, pl.ds(group + GROUPS, 1), :] = jnp.sum(value_acc[...], axis=0, keepdims=True)
        for at in range(0, width, span):
            acc[at : at + span, :] = product(left_t[at : at + span, :], joined[...])
        finish(3, r)
        w_load(r).wait()
        for at in range(0, rows, chunk):
            tokens[at : at + chunk, :] += contract_cols(joined[at : at + chunk, :], w_in[...])
        pl.when(r < 3)(lambda: w_load(r + 1).start())
        return carry

    lax.fori_loop(0, GROUPS, group_step, 0)
    sums_copy(1, 0).start()
    pl.when(c == 0)(lambda: pass_first(3))
    swap = remote_copy(
        tokens.at[pl.ds(half_rows, half_rows)], tokens_out.at[c], swap_sem.at[0], swap_sem.at[1], partner
    )
    keep = pltpu.make_async_copy(tokens.at[pl.ds(0, half_rows)], tokens_out.at[c], load_sem.at[4])
    swap.start()
    keep.start()
    sums_step(1, 0)
    take_second(3, 0)
    sums_step(1, 1)
    take_z(1)
    take_first(3)
    sums_step(1, 2)
    take_z(2)
    take_z(3)
    sums_last(1)
    keep.wait()
    swap.wait()
    for p in range(BIG):
        for r in range(2):
            core_copy(p, r).wait_send()
            second_copy(p, r).wait_send()
        first_copy(p).wait_send()
        for d in range(nz - 1):
            z_copy(p, d).wait_send()
    for v in range(2):
        for k in range(nz + 2):
            sums_copy(v, k).wait_send()


def todo_of(todo):
    def run():
        todo()

    return run


def backward(info, lse, dense_sums, *operands):
    rows_in, w_joined = operands[:2]
    nz = lax.axis_size("dp") // 2
    rows, width = rows_in.shape
    low, wide = jnp.bfloat16, jnp.float32
    deep = width // (2 * nz)
    tails = [(deep, width), (deep, width), (GC // (2 * nz), width), (deep, 3 * GC)]
    results = [*tails[:3], *[(deep, GC)] * 3]
    sums = [dense_sums.shape, (2 * GROUPS, PAD)]
    anywhere, vmem = pl.BlockSpec(memory_space=pl.ANY), pl.BlockSpec(memory_space=pltpu.VMEM)
    dma = pltpu.SemaphoreType.DMA
    return pl.pallas_call(
        functools.partial(backward_kernel, nz),
        in_specs=[pl.BlockSpec(memory_space=pltpu.SMEM), vmem, vmem, *[anywhere] * len(operands)],
        out_specs=[*[vmem] * 8, anywhere],
        out_shape=[
            *[jax.ShapeDtypeStruct(shape, wide) for shape in (*results, *sums)],
            jax.ShapeDtypeStruct((MB, rows // 2, width), wide),
        ],
        scratch_shapes=[
            *[pltpu.VMEM((2, 2, nz, 2, *t), low) for t in tails],
            *[pltpu.VMEM((2, nz, 2, *t), low) for t in tails],
            *[pltpu.VMEM((2, nz, *t), low) for t in tails],
            *[pltpu.VMEM((nz, *t), low) for t in tails],
            *[pltpu.VMEM((nz - 1, *t), low) for t in tails],
            *[pltpu.VMEM((4, *shape), wide) for shape in sums],
            *[pltpu.VMEM((nz + 2, *shape), wide) for shape in sums],
            pltpu.VMEM((width, 3 * PAD), wide),
            pltpu.VMEM((2, rows, width), low),
            pltpu.VMEM((rows, width), low),
            pltpu.VMEM((width, rows), low),
            pltpu.VMEM((rows, 3 * PAD), low),
            pltpu.VMEM((2, rows, PAD), low),
            pltpu.VMEM((2, rows, PAD), low),
            pltpu.VMEM((width, 3 * PAD), low),
            pltpu.VMEM((rows, width), wide),
            pltpu.VMEM((rows, rows), low),
            pltpu.VMEM((rows, rows), low),
            pltpu.VMEM((PAD, rows), wide),
            pltpu.VMEM((PAD, rows), wide),
            pltpu.VMEM((PAD, rows), low),
            pltpu.VMEM((rows, PAD), wide),
            pltpu.VMEM((rows, PAD), wide),
            dma((BIG, 5)),
            dma((BIG, 5)),
            dma((BIG, nz - 1)),
            dma((BIG, nz - 1)),
            dma((2, nz + 2)),
            dma((2, nz + 2)),
            dma((2,)),
            dma((5,)),
            dma((2,)),
            dma((2,)),
            dma((2,)),
        ],
        compiler_params=pltpu.CompilerParams(
            collective_id=1, has_side_effects=True, vmem_limit_bytes=63 * 1024 * 1024
        ),
    )(info, lse, dense_sums, *operands)


def body_fused(
    tokens,
    cotangent,
    lengths,
    w_query,
    w_key,
    w_value,
    w_out,
    w_up,
    w_down,
    b_query,
    b_value,
    b_up,
    b_out,
    b_down,
    norm1_gain,
    norm1_shift,
    norm2_gain,
    norm2_shift,
):
    half_rows = tokens.shape[1]
    width = tokens.shape[2]
    n_dp, n_mp = lax.axis_size("dp"), lax.axis_size("mp")
    unit_cols = w_up.shape[1]
    mp_index = lax.axis_index("mp")
    half = lax.rem(mp_index, 2)
    seq = lax.div(mp_index, 2)

    length = lax.dynamic_slice(lengths, (half, seq), (1, 1))[0, 0]
    info = jnp.stack([length, half])
    mark = jnp.zeros((PAD - GC,), jnp.float32).at[0].set(1.0)
    bias_rows = jnp.concatenate(
        [b_query, mark, jnp.zeros((PAD,), jnp.float32), b_value, jnp.zeros((PAD - GC,), jnp.float32), b_up]
    ).reshape(2, width)
    bias_rows = jnp.pad(bias_rows, ((0, 6), (0, 0)))
    qkv_shard = jnp.concatenate([w_query, w_key, w_value], axis=1)
    gathered = forward_attention(
        lengths, tokens, cotangent, (qkv_shard, w_out, w_up, w_down), bias_rows
    )
    full_out, full_up, full_down = (
        g.reshape(n_mp, n_dp * g.shape[4], g.shape[5]) for g in gathered[1:4]
    )
    full_bias, rows_in, rows_cot, w_joined, qkv, heads, lse = gathered[4:]
    out_pad = jnp.pad(full_out, ((0, 0), (0, PAD - GC), (0, 0))).reshape(n_mp * PAD, width)
    vecs = jnp.stack([b_out, b_down, norm1_gain, norm1_shift, norm2_gain, norm2_shift, b_out, b_out])
    (
        output,
        first_low,
        active,
        ffn_grad_low,
        preact_low,
        attn_grad,
        attn_grad_low,
        heads_grad,
        dense_sums,
    ) = dense(info, heads, rows_in, rows_cot, out_pad, full_up, full_down, vecs, full_bias)
    *matrix_grads, dense_total, head_total, tokens_grad = backward(
        info,
        lse,
        dense_sums,
        rows_in,
        w_joined,
        attn_grad,
        qkv,
        heads,
        heads_grad,
        active,
        ffn_grad_low,
        first_low,
        preact_low,
        attn_grad_low,
    )
    own_down, own_up, own_out, own_query, own_key, own_value = matrix_grads
    dp_index = lax.axis_index("dp")

    def piece(values, row, index, size):
        return lax.dynamic_slice(values, (row, index * size), (1, size))[0]

    share = width // (n_dp * n_mp)
    bias_grads = [piece(head_total, at + mp_index, dp_index, share) for at in (0, GROUPS)]
    bias_grads.append(piece(dense_total, 12 + mp_index, dp_index, unit_cols // n_dp))
    vector_grads = lax.dynamic_slice(dense_total, (0, (dp_index * n_mp + mp_index) * share), (6, share))
    squares = jnp.sum(dense_total[6:9], axis=1)
    rms_values = jnp.sqrt(squares / (dense_total[9, 0] * width))

    def back_home(rows):
        mine, sent = rows[:half_rows], swap_with_partner(rows[half_rows:])
        return jnp.where(half == 0, jnp.stack([mine, sent]), jnp.stack([sent, mine]))

    return (
        back_home(output),
        tokens_grad,
        own_query,
        own_key,
        own_value,
        own_out,
        own_up,
        own_down,
        *bias_grads,
        *vector_grads,
        rms_values,
    )


def solution(mesh):
    rows = P(None, BOTH, None)
    split, rows_split = P("dp", "mp"), P(("mp", "dp"), None)
    aligned = mesh.shape["dp"] == 8 and mesh.shape["mp"] == 4
    return jax.shard_map(
        body_fused if aligned else body_any,
        mesh=mesh,
        in_specs=(
            rows,
            rows,
            P(None, "dp"),
            split,
            split,
            split,
            rows_split,
            split,
            rows_split,
            P("mp"),
            P("mp"),
            P("mp"),
            *([P()] * 6),
        ),
        out_specs=(
            rows,
            rows,
            split,
            split,
            split,
            rows_split,
            split,
            rows_split,
            *([P(("mp", "dp"))] * 3),
            *([P(BOTH)] * 6),
            P(),
        ),
        check_vma=False,
    )
```

profile of v0, /device:TPU:0, one launch (start us, length us, event | category | flops | bytes accessed | tf_op | source)
XLA Modules:
  0.0 275.5 jit_solution(11164032963588305311)
XLA Ops:
  0.7 0.8 concatenate.9
  1.5 0.6 pad.10.bias_shard
  2.1 0.7 stack.45
  2.8 0.7 stack.46
  3.5 0.7 stack.47
  4.2 0.7 stack.48
  4.9 0.7 stack.49
  5.6 0.7 stack.50
  6.3 1.3 dynamic_slice.15
  7.5 1.2 pad_add_fusion.info_ref.info
  8.8 1.6 pad_maximum_fusion.shard_q
  10.3 93.0 %shard_map.313 = (bf16[2,2,4,2,96,576]{5,4,3,2,1,0:T(8,128)(2,1)}, bf16[2,2,4,2,24,768]{5,4,3,2,1,0:T(8,128)(2,1)}, bf16[2,2,4,2,96,768]{5,4,3,2,1,0:T(8,128)(2,...) custom-call(s32[2,2]{1,0:T(2,128)} %lengths.1, ...), custom_call_target="tpu_custom_call" | custom-call | tf_op jit(solution)/shard_map/pallas_call | solution.py:962
  103.3 2.5 pad.11
  105.8 0.6 stack.51.vec_ref
  106.5 38.0 %shard_map.314 = (bf16[1024,768]{1,0:T(8,128)(2,1)}, bf16[1024,768]{1,0:T(8,128)(2,1)}, bf16[1024,3072]{1,0:T(8,128)(2,1)}, bf16[1024,768]{1,0:T(8,128)(2,1)}, b...) custom-call(s32[2]{0:T(128)} %pad_add_fusion.info_ref.info, ...), custom_call_target="tpu_custom_call" | custom-call | flops 22599999488 | bytes 40000000 | tf_op jit(solution)/shard_map/pallas_call | solution.py:1119
  144.5 2.4 slice_bitcast_fusion
  146.9 0.6 collective-permute-start
  147.4 112.7 %shard_map.315 = (f32[96,768]{1,0:T(8,128)}, f32[96,768]{1,0:T(8,128)}, f32[24,768]{1,0:T(8,128)}, f32[96,192]{1,0:T(8,128)}, f32[96,192]{1,0:T(8,128)}, /*index...) custom-call(s32[2]{0:T(128)} %pad_add_fusion.info_ref.info, ...), custom_call_target="tpu_custom_call" | custom-call | tf_op jit(solution)/shard_map/pallas_call | solution.py:1541
  260.1 1.2 slice.24
  262.0 1.3 dynamic-slice_bitcast_fusion
  263.3 0.8 constant_dynamic-slice_fusion
  264.0 0.9 slice_reduce_fusion
  265.0 0.5 divide_sqrt_fusion
  265.5 1.4 slice_bitcast_fusion.1
  266.9 2.9 %maximum_select_fusion = bf16[2,512,768]{2,1,0:T(8,128)(2,1)} fusion(bf16[1,512,768]{2,1,0:T(8,128)(2,1)} %bitcast.7, bf16[1,512,768]{2,1,0:T(8,128)(2,1)S(1)} %get-tuple-element.86, pred[]{:T(512)S(6)} %eq.3), kind=kLoop, calls=%fused_computation | loop fusion | flops 2359296 | bytes 3145729 | tf_op jit(solution)/shard_map/jit(_where)/select_n | solution.py:1678
  269.8 1.7 copy.43
  271.5 0.6 copy.44
  272.1 0.6 copy.45
  272.8 0.6 copy.46
  273.4 0.6 copy.47
  274.0 0.7 copy.48
  274.8 0.7 copy.49
  (18 shorter events, 0.0 us)
Async XLA Ops:
  146.9 120.0 %collective-permute-start = (bf16[512,768]{1,0:T(8,128)(2,1)}, bf16[512,768]{1,0:T(8,128)(2,1)}, u32[]{:S(2)}, u32[]{:S(2)}) collective-permute-start(bf16[512,768]{1,0:T(8,128)(2,1)} %get-tuple-element.87), channel_id=1, source_target_pairs={{0,1},{1,0},{2,3},{3,2},{4,5},{5,4},{6,7},{7,6},{8,9},{9,8},{10,11... | collective-permute-start | bytes 2359304 | tf_op jit(solution)/shard_map/ppermute | solution.py:190
  266.9 2.9 %copy-start = (f32[2,512,768]{2,1,0:T(8,128)S(1)}, f32[2,512,768]{2,1,0:T(8,128)}, u32[]{:S(2)}) copy-start(f32[2,512,768]{2,1,0:T(8,128)} %get-tuple-element.117) | copy-start | bytes 9437188
  269.8 1.7 copy-start.5
  269.8 2.4 copy-start.4
  269.8 3.0 %copy-start.3 = (f32[96,192]{1,0:T(8,128)S(1)}, f32[96,192]{1,0:T(8,128)}, u32[]{:S(2)}) copy-start(f32[96,192]{1,0:T(8,128)} %get-tuple-element.120) | copy-start | bytes 221188
  269.8 3.6 %copy-start.6 = (f32[24,768]{1,0:T(8,128)S(1)}, f32[24,768]{1,0:T(8,128)}, u32[]{:S(2)}) copy-start(f32[24,768]{1,0:T(8,128)} %get-tuple-element.121) | copy-start | bytes 221188
  269.8 4.3 %copy-start.2 = (f32[96,768]{1,0:T(8,128)S(1)}, f32[96,768]{1,0:T(8,128)}, u32[]{:S(2)}) copy-start(f32[96,768]{1,0:T(8,128)} %get-tuple-element.122) | copy-start | bytes 884740
  269.8 5.0 %copy-start.1 = (f32[96,768]{1,0:T(8,128)S(1)}, f32[96,768]{1,0:T(8,128)}, u32[]{:S(2)}) copy-start(f32[96,768]{1,0:T(8,128)} %get-tuple-element.123) | copy-start | bytes 884740
where the time goes:
time: 277 us; the launch traced here: 275 us
  Pallas kernels  244 us (88%)
  local copies, waits for them, and re-layouts  22.7 us (8%)
  other arithmetic  7.16 us (3%)
    pallas_call x1, Pallas kernels, backward(): pl.pallas_call(functools.partial(backward_kernel, nz), in_specs=[pl.Block...  113 us
    pallas_call x1, Pallas kernels, forward_attention(): pl.pallas_call(functools.partial(forward_kernel, nz), in_specs=[pl.BlockS...  93 us
    pallas_call x1, Pallas kernels, dense(): pl.pallas_call(dense_kernel, grid=(count // tile,), in_specs=[pl.BlockSpe...  38 us
    unnamed x21, local copies, waits for them, and re-layouts  5.68 us
  transfers between devices with their start and end apart: 1, of which 0 were waited for; matrix products, arithmetic and copies ran while one was open for 2% of the time, Pallas kernels for 41%

commit v1 on v0

--- a/solution.py
+++ b/solution.py
@@ -656,7 +656,9 @@
     lengths,
     tokens,
     cotangent,
-    shard_q,
+    shard_wq,
+    shard_wk,
+    shard_wv,
     shard_o,
     shard_u,
     shard_d,
@@ -672,6 +674,7 @@
     qkv_out,
     heads_out,
     lse_out,
+    shard_q,
     rows,
     cots,
     w_got,
@@ -704,6 +707,8 @@
     slanted = at_place(1 - x, 1 - c, z, y)
     own, got1, got2, got3 = regions(x, c, y)
     other = regions(x, 1 - c, y)
+    for k, shard in enumerate((shard_wq, shard_wk, shard_wv)):
+        shard_q[:, k * GC : (k + 1) * GC] = shard[...]
     meet([first, second, partner, slanted, *along])
 
     def block(p, core, place, d):
@@ -957,14 +962,18 @@
     half_rows, width = tokens.shape[1:]
     rows = 2 * half_rows
     low = jnp.bfloat16
+    joined_shape = (shards[0].shape[0], 3 * GC)
     anywhere, vmem = pl.BlockSpec(memory_space=pl.ANY), pl.BlockSpec(memory_space=pltpu.VMEM)
     dma = pltpu.SemaphoreType.DMA
     return pl.pallas_call(
         functools.partial(forward_kernel, nz),
-        in_specs=[pl.BlockSpec(memory_space=pltpu.SMEM), anywhere, anywhere, *[vmem] * 5],
+        in_specs=[pl.BlockSpec(memory_space=pltpu.SMEM), anywhere, anywhere, *[vmem] * 7],
         out_specs=[*[anywhere] * PARTS, vmem, *[anywhere] * 5, vmem],
         out_shape=[
-            *[jax.ShapeDtypeStruct((2, 2, nz, 2, *s.shape), s.dtype) for s in shards],
+            *[
+                jax.ShapeDtypeStruct((2, 2, nz, 2, *shape), low)
+                for shape in (joined_shape, *[s.shape for s in shards[3:]])
+            ],
             jax.ShapeDtypeStruct((GROUPS, *bias_shard.shape), jnp.float32),
             jax.ShapeDtypeStruct((rows, width), low),
             jax.ShapeDtypeStruct((rows, width), low),
@@ -974,9 +983,10 @@
             jax.ShapeDtypeStruct((GROUPS, 8, rows), jnp.float32),
         ],
         scratch_shapes=[
+            pltpu.VMEM(joined_shape, low),
             pltpu.VMEM((rows, width), low),
             pltpu.VMEM((rows, width), low),
-            pltpu.VMEM((nz, 2, *shards[0].shape), low),
+            pltpu.VMEM((nz, 2, *joined_shape), low),
             pltpu.VMEM((width, 3 * PAD), low),
             pltpu.VMEM((rows, 3 * PAD), low),
             pltpu.VMEM((PAD, rows), low),
@@ -1000,20 +1010,18 @@
     )(lengths, tokens, cotangent, *shards, bias_shard)
 
 
-def place_of(info_ref, row, half_rows):
-    half = info_ref[1]
+def place_of(half, row, half_rows):
     return jnp.where(row < half_rows, row + half * half_rows, row - half * half_rows)
 
 
 def dense_kernel(
-    info_ref,
+    lengths,
     heads_ref,
     rows_ref,
     cot_ref,
-    out_w,
-    up_w,
-    down_w,
-    vec_ref,
+    out_full,
+    up_full,
+    down_full,
     bias_ref,
     output_ref,
     first_ref,
@@ -1025,26 +1033,53 @@
     heads_grad_ref,
     sums_ref,
     slope,
+    out_pad,
+    up_w,
+    down_w,
+    load_sem,
 ):
     t = pl.program_id(0)
+    mp = lax.axis_index("mp")
+    half, seq = lax.rem(mp, 2), lax.div(mp, 2)
     low = jnp.bfloat16
     tile, width = rows_ref.shape
     units = up_w.shape[2]
-    b_out, b_down, gain1, shift1, gain2, shift2 = (vec_ref[k : k + 1, :] for k in range(6))
+    b_out, b_down, gain1, shift1, gain2, shift2 = (
+        bias_ref[0, 2 + k : 3 + k, :] for k in range(6)
+    )
+    out_load = pltpu.make_async_copy(out_full, out_pad.at[:, pl.ds(0, GC), :], load_sem.at[2 * GROUPS])
+    up_loads = [pltpu.make_async_copy(up_full.at[g], up_w.at[g], load_sem.at[g]) for g in range(GROUPS)]
+    down_loads = [
+        pltpu.make_async_copy(down_full.at[g], down_w.at[g], load_sem.at[GROUPS + g]) for g in range(GROUPS)
+    ]
 
     @pl.when(t == 0)
     def _():
+        out_load.start()
+        for g in range(GROUPS):
+            up_loads[g].start()
+            down_loads[g].start()
+        out_pad[:, GC:, :] = jnp.zeros((GROUPS, PAD - GC, width), low)
         sums_ref[...] = jnp.zeros_like(sums_ref)
+        out_load.wait()
+
+    out_w = out_pad[...].reshape(GROUPS * PAD, width)
 
     def count(k, values):
         sums_ref[k : k + 1, :] += jnp.sum(values, axis=0, keepdims=True)
 
-    attention = product(heads_ref[...], out_w[...]) + b_out
+    attention = product(heads_ref[...], out_w) + b_out
     first_norm, first_scaled, first_inverse = layer_norm(
         rows_ref[...].astype(jnp.float32) + attention, gain1, shift1
     )
     first_low = first_norm.astype(low)
     first_ref[...] = first_low
+
+    @pl.when(t == 0)
+    def _():
+        for copy in (*up_loads, *down_loads):
+            copy.wait()
+
     ffn_out = jnp.broadcast_to(b_down, (tile, width))
     for g in range(GROUPS):
         preact = product(first_low, up_w[g]) + bias_ref[g, 1:2, :]
@@ -1057,7 +1092,7 @@
         ffn_out = ffn_out + product(active, down_w[g])
     stream = first_norm + ffn_out
     row = lax.broadcasted_iota(jnp.int32, (tile, 1), 0) + t * tile
-    valid = (place_of(info_ref, row, pl.num_programs(0) * tile // 2) < info_ref[0]).astype(jnp.float32)
+    valid = (place_of(half, row, pl.num_programs(0) * tile // 2) < lengths[half, seq]).astype(jnp.float32)
     count(6, valid * stream * stream)
     count(7, valid * attention * attention)
     count(8, valid * ffn_out * ffn_out)
@@ -1091,10 +1126,10 @@
     attn_ref[...] = attn_grad
     attn_grad_low = attn_grad.astype(low)
     attn_low_ref[...] = attn_grad_low
-    heads_grad_ref[...] = contract_cols(attn_grad_low, out_w[...]).astype(low)
-
-
-def dense(info, heads, rows, cots, out_w, up_w, down_w, vecs, biases):
+    heads_grad_ref[...] = contract_cols(attn_grad_low, out_w).astype(low)
+
+
+def dense(lengths, heads, rows, cots, out_w, up_w, down_w, biases):
     count, width = rows.shape
     tile = 256
     units = up_w.shape[2]
@@ -1124,10 +1159,7 @@
             tiled(GROUPS * PAD),
             tiled(width),
             tiled(width),
-            whole(out_w.shape),
-            whole(up_w.shape),
-            whole(down_w.shape),
-            whole(vecs.shape),
+            *[pl.BlockSpec(memory_space=pl.ANY)] * 3,
             whole(biases.shape),
         ],
         out_specs=[*[tiled(columns) for columns, _ in outs], whole((16, width))],
@@ -1135,11 +1167,17 @@
             *[jax.ShapeDtypeStruct((count, columns), kind) for columns, kind in outs],
             jax.ShapeDtypeStruct((16, width), jnp.float32),
         ],
-        scratch_shapes=[pltpu.VMEM((tile, GROUPS * units), jnp.float32)],
+        scratch_shapes=[
+            pltpu.VMEM((tile, GROUPS * units), jnp.float32),
+            pltpu.VMEM((GROUPS, PAD, width), low),
+            pltpu.VMEM(up_w.shape, low),
+            pltpu.VMEM(down_w.shape, low),
+            pltpu.SemaphoreType.DMA((2 * GROUPS + 1,)),
+        ],
         cost_estimate=pl.CostEstimate(
             flops=22_600_000_000, bytes_accessed=40_000_000, transcendentals=7_000_000
         ),
-    )(info, heads, rows, cots, out_w, up_w, down_w, vecs, biases)
+    )(lengths, heads, rows, cots, out_w, up_w, down_w, biases)
 
 
 BIG = 4
@@ -1147,7 +1185,7 @@
 
 def backward_kernel(
     nz,
-    info,
+    lengths,
     lse_ref,
     dense_sums,
     rows_in,
@@ -1161,19 +1199,22 @@
     first_low,
     preact_low,
     attn_low,
+    normed,
     down_out,
     up_out,
     out_out,
     query_out,
     key_out,
     value_out,
-    dense_total,
-    head_total,
+    vectors_out,
     tokens_out,
+    normed_out,
     *refs,
 ):
     parts, heard1, heard2, heard3, heard4 = (refs[BIG * i : BIG * (i + 1)] for i in range(5))
     (
+        dense_total,
+        head_total,
         dense_kept,
         head_kept,
         dense_heard,
@@ -1367,8 +1408,12 @@
     first_load.start()
     w_load(0).start()
     tokens_load.start()
+    dense_kept[0] = dense_sums[...]
     meet([first, second, partner, *along])
-    dense_kept[0] = dense_sums[...]
+    normed_swap = remote_copy(
+        normed.at[pl.ds(half_rows, half_rows)], normed_out, swap_sem.at[2], swap_sem.at[3], partner
+    )
+    normed_swap.start()
     ffn_load.wait()
 
     def down_step(r, carry):
@@ -1428,7 +1473,7 @@
         11: lambda: pl.when(c == 1)(lambda: pass_first(3)),
     }
     row = lax.broadcasted_iota(jnp.int32, (rows, 1), 0)
-    bias = jnp.where(place_of(info, row, half_rows) < info[0], 0.0, masked_score).astype(low)
+    bias = jnp.where(place_of(c, row, half_rows) < lengths[c, x], 0.0, masked_score).astype(low)
     lane = lax.broadcasted_iota(jnp.int32, (1, PAD), 1)
     turned[...] = jnp.zeros_like(turned)
 
@@ -1497,6 +1542,22 @@
     keep = pltpu.make_async_copy(tokens.at[pl.ds(0, half_rows)], tokens_out.at[c], load_sem.at[4])
     swap.start()
     keep.start()
+
+    def piece(values, index, count):
+        size = values.shape[1] // count
+        found = values[:, :size]
+        for k in range(1, count):
+            found = jnp.where(index == k, values[:, k * size : (k + 1) * size], found)
+        return found
+
+    dp = 2 * z + y
+    vectors_out[...] = jnp.zeros_like(vectors_out)
+    share = width // (8 * nz)
+    vectors_out[0:6, :share] = piece(dense_total[0:6, :], dp * 4 + mp, 8 * nz)
+    vectors_out[6:7, : width // (2 * nz)] = piece(dense_total[pl.ds(12 + mp, 1), :], dp, 2 * nz)
+    for k in range(3):
+        square = jnp.sum(dense_total[6 + k : 7 + k, :], axis=1, keepdims=True)
+        vectors_out[12:13, k : k + 1] = jnp.sqrt(square / (dense_total[9:10, 0:1] * width))
     sums_step(1, 0)
     take_second(3, 0)
     sums_step(1, 1)
@@ -1506,8 +1567,12 @@
     take_z(2)
     take_z(3)
     sums_last(1)
+
+    vectors_out[7:8, :share] = piece(head_total[pl.ds(mp, 1), :GC], dp, 2 * nz)
+    vectors_out[8:9, :share] = piece(head_total[pl.ds(mp + GROUPS, 1), :GC], dp, 2 * nz)
     keep.wait()
     swap.wait()
+    normed_swap.wait()
     for p in range(BIG):
         for r in range(2):
             core_copy(p, r).wait_send()
@@ -1527,7 +1592,7 @@
     return run
 
 
-def backward(info, lse, dense_sums, *operands):
+def backward(lengths, lse, dense_sums, *operands):
     rows_in, w_joined = operands[:2]
     nz = lax.axis_size("dp") // 2
     rows, width = rows_in.shape
@@ -1541,10 +1606,11 @@
     return pl.pallas_call(
         functools.partial(backward_kernel, nz),
         in_specs=[pl.BlockSpec(memory_space=pltpu.SMEM), vmem, vmem, *[anywhere] * len(operands)],
-        out_specs=[*[vmem] * 8, anywhere],
+        out_specs=[*[vmem] * 7, anywhere, anywhere],
         out_shape=[
-            *[jax.ShapeDtypeStruct(shape, wide) for shape in (*results, *sums)],
+            *[jax.ShapeDtypeStruct(shape, wide) for shape in (*results, (16, 128))],
             jax.ShapeDtypeStruct((MB, rows // 2, width), wide),
+            jax.ShapeDtypeStruct((rows // 2, width), low),
         ],
         scratch_shapes=[
             *[pltpu.VMEM((2, 2, nz, 2, *t), low) for t in tails],
@@ -1552,6 +1618,7 @@
             *[pltpu.VMEM((2, nz, *t), low) for t in tails],
             *[pltpu.VMEM((nz, *t), low) for t in tails],
             *[pltpu.VMEM((nz - 1, *t), low) for t in tails],
+            *[pltpu.VMEM(shape, wide) for shape in sums],
             *[pltpu.VMEM((4, *shape), wide) for shape in sums],
             *[pltpu.VMEM((nz + 2, *shape), wide) for shape in sums],
             pltpu.VMEM((width, 3 * PAD), wide),
@@ -1576,7 +1643,7 @@
             dma((BIG, nz - 1)),
             dma((2, nz + 2)),
             dma((2, nz + 2)),
-            dma((2,)),
+            dma((4,)),
             dma((5,)),
             dma((2,)),
             dma((2,)),
@@ -1585,7 +1652,7 @@
         compiler_params=pltpu.CompilerParams(
             collective_id=1, has_side_effects=True, vmem_limit_bytes=63 * 1024 * 1024
         ),
-    )(info, lse, dense_sums, *operands)
+    )(lengths, lse, dense_sums, *operands)
 
 
 def body_fused(
@@ -1612,27 +1679,30 @@
     width = tokens.shape[2]
     n_dp, n_mp = lax.axis_size("dp"), lax.axis_size("mp")
     unit_cols = w_up.shape[1]
-    mp_index = lax.axis_index("mp")
-    half = lax.rem(mp_index, 2)
-    seq = lax.div(mp_index, 2)
-
-    length = lax.dynamic_slice(lengths, (half, seq), (1, 1))[0, 0]
-    info = jnp.stack([length, half])
     mark = jnp.zeros((PAD - GC,), jnp.float32).at[0].set(1.0)
     bias_rows = jnp.concatenate(
-        [b_query, mark, jnp.zeros((PAD,), jnp.float32), b_value, jnp.zeros((PAD - GC,), jnp.float32), b_up]
-    ).reshape(2, width)
-    bias_rows = jnp.pad(bias_rows, ((0, 6), (0, 0)))
-    qkv_shard = jnp.concatenate([w_query, w_key, w_value], axis=1)
+        [
+            b_query,
+            mark,
+            jnp.zeros((PAD,), jnp.float32),
+            b_value,
+            jnp.zeros((PAD - GC,), jnp.float32),
+            b_up,
+            b_out,
+            b_down,
+            norm1_gain,
+            norm1_shift,
+            norm2_gain,
+            norm2_shift,
+        ]
+    ).reshape(8, width)
     gathered = forward_attention(
-        lengths, tokens, cotangent, (qkv_shard, w_out, w_up, w_down), bias_rows
+        lengths, tokens, cotangent, (w_query, w_key, w_value, w_out, w_up, w_down), bias_rows
     )
     full_out, full_up, full_down = (
         g.reshape(n_mp, n_dp * g.shape[4], g.shape[5]) for g in gathered[1:4]
     )
     full_bias, rows_in, rows_cot, w_joined, qkv, heads, lse = gathered[4:]
-    out_pad = jnp.pad(full_out, ((0, 0), (0, PAD - GC), (0, 0))).reshape(n_mp * PAD, width)
-    vecs = jnp.stack([b_out, b_down, norm1_gain, norm1_shift, norm2_gain, norm2_shift, b_out, b_out])
     (
         output,
         first_low,
@@ -1643,9 +1713,9 @@
         attn_grad_low,
         heads_grad,
         dense_sums,
-    ) = dense(info, heads, rows_in, rows_cot, out_pad, full_up, full_down, vecs, full_bias)
-    *matrix_grads, dense_total, head_total, tokens_grad = backward(
-        info,
+    ) = dense(lengths, heads, rows_in, rows_cot, full_out, full_up, full_down, full_bias)
+    *matrix_grads, vectors, tokens_grad, output_got = backward(
+        lengths,
         lse,
         dense_sums,
         rows_in,
@@ -1659,26 +1729,15 @@
         first_low,
         preact_low,
         attn_grad_low,
-    )
-    own_down, own_up, own_out, own_query, own_key, own_value = matrix_grads
-    dp_index = lax.axis_index("dp")
-
-    def piece(values, row, index, size):
-        return lax.dynamic_slice(values, (row, index * size), (1, size))[0]
-
+        output,
+    )
     share = width // (n_dp * n_mp)
-    bias_grads = [piece(head_total, at + mp_index, dp_index, share) for at in (0, GROUPS)]
-    bias_grads.append(piece(dense_total, 12 + mp_index, dp_index, unit_cols // n_dp))
-    vector_grads = lax.dynamic_slice(dense_total, (0, (dp_index * n_mp + mp_index) * share), (6, share))
-    squares = jnp.sum(dense_total[6:9], axis=1)
-    rms_values = jnp.sqrt(squares / (dense_total[9, 0] * width))
-
-    def back_home(rows):
-        mine, sent = rows[:half_rows], swap_with_partner(rows[half_rows:])
-        return jnp.where(half == 0, jnp.stack([mine, sent]), jnp.stack([sent, mine]))
-
+    sizes = [*[share] * 6, unit_cols // n_dp, share, share, 3]
+    delivered = deliver(matrix_grads, vectors, output, output_got, tokens_grad, sizes)
+    output, tokens_grad, own_down, own_up, own_out, own_query, own_key, own_value = delivered[:8]
+    own_vectors = [v.reshape(-1) for v in delivered[8:]]
     return (
-        back_home(output),
+        output,
         tokens_grad,
         own_query,
         own_key,
@@ -1686,10 +1745,67 @@
         own_out,
         own_up,
         own_down,
-        *bias_grads,
-        *vector_grads,
-        rms_values,
-    )
+        own_vectors[7],
+        own_vectors[8],
+        own_vectors[6],
+        *own_vectors[:6],
+        own_vectors[9],
+    )
+
+
+def deliver_kernel(mats, *refs):
+    results, (vectors, normed, normed_got, tokens) = refs[:mats], refs[mats : mats + 4]
+    outs = refs[mats + 4 :]
+    normed_out, tokens_out = outs[:2]
+    mat_outs, vec_outs = outs[2 : 2 + mats], outs[2 + mats : 12 + mats]
+    normed_kept, tokens_kept, load_sem, store_sem = outs[12 + mats :]
+    half = lax.rem(lax.axis_index("mp"), 2)
+    half_rows = tokens.shape[1]
+    moves = [
+        (tokens.at[0], tokens_kept.at[0], tokens_out.at[0]),
+        (tokens.at[1], tokens_kept.at[1], tokens_out.at[1]),
+        (normed.at[pl.ds(0, half_rows)], normed_kept.at[0], normed_out.at[half]),
+        (normed_got, normed_kept.at[1], normed_out.at[1 - half]),
+    ]
+    loads = [pltpu.make_async_copy(a, b, load_sem.at[k]) for k, (a, b, _) in enumerate(moves)]
+    stores = [pltpu.make_async_copy(b, o, store_sem.at[k]) for k, (_, b, o) in enumerate(moves)]
+    stores += [
+        pltpu.make_async_copy(a, o, store_sem.at[len(moves) + k])
+        for k, (a, o) in enumerate(zip(results, mat_outs))
+    ]
+    for copy in (*loads, *stores[len(moves) :]):
+        copy.start()
+    for k, out in enumerate(vec_outs[:9]):
+        out[...] = vectors[k : k + 1, : out.shape[1]]
+    vec_outs[9][...] = vectors[12:13, :3]
+    for k, copy in enumerate(loads):
+        copy.wait()
+        stores[k].start()
+    for copy in stores:
+        copy.wait()
+
+
+def deliver(results, vectors, normed, normed_got, tokens, sizes):
+    mats = len(results)
+    anywhere, vmem = pl.BlockSpec(memory_space=pl.ANY), pl.BlockSpec(memory_space=pltpu.VMEM)
+    big = [jax.ShapeDtypeStruct((2, *normed_got.shape), normed.dtype), jax.ShapeDtypeStruct(tokens.shape, tokens.dtype)]
+    rows = [jax.ShapeDtypeStruct((1, size), jnp.float32) for size in sizes]
+    return pl.pallas_call(
+        functools.partial(deliver_kernel, mats),
+        grid=(1,),
+        in_specs=[*[vmem] * (mats + 1), *[anywhere] * 3],
+        out_specs=[
+            *[anywhere] * (2 + mats),
+            *[pl.BlockSpec((1, size), lambda i: (0, 0)) for size in sizes],
+        ],
+        out_shape=[*big, *[jax.ShapeDtypeStruct(r.shape, r.dtype) for r in results], *rows],
+        scratch_shapes=[
+            pltpu.VMEM(big[0].shape, big[0].dtype),
+            pltpu.VMEM(big[1].shape, big[1].dtype),
+            pltpu.SemaphoreType.DMA((4,)),
+            pltpu.SemaphoreType.DMA((4 + mats,)),
+        ],
+    )(*results, vectors, normed, normed_got, tokens)
 
 
 def solution(mesh):

time: 277 us -> 255 us (0.921)
  local copies, waits for them, and re-layouts: 22.7 us -> 1.52 us
  Pallas kernels: 244 us -> 252 us
  other arithmetic: 7.16 us -> 0 us
    another operation x10 -> x1, local copies, waits for them, and re-layouts: 8.5 us -> 0.01 us  [the longest x7 4.78 us: body_fused(): jnp.stack([b_out, b_down, norm1_gain, norm1_shift, norm2_gain, norm2_shif...]
    pallas_call x0 -> x1, Pallas kernels: none -> 5.82 us  [deliver(): pl.pallas_call(functools.partial(deliver_kernel, mats), grid=(1,), in_spe...]
    unnamed x21 -> x0, local copies, waits for them, and re-layouts: 5.68 us -> none
    pad x2 -> x0, local copies, waits for them, and re-layouts: 3.13 us -> none  [the longest x1 2.52 us: body_fused(): jnp.pad(full_out, ((0, 0), (0, PAD - GC), (0, 0)))]
    select_n x1 -> x0, other arithmetic: 2.9 us -> none  [back_home(): jnp.where(half == 0, jnp.stack([mine, sent]), jnp.stack([sent, mine]))]
  transfers between devices with their start and end apart: 1 -> 0, of which waited for: 0 -> 0; matrix products, arithmetic and copies ran while one was open for 2% -> 0% of each run, Pallas kernels for 41% -> 0%
where the time goes in v1:
time: 255 us; the launch traced here: 254 us
  Pallas kernels  252 us (99%)
    pallas_call x1, Pallas kernels, backward(): pl.pallas_call(functools.partial(backward_kernel, nz), in_specs=[pl.Block...  114 us
    pallas_call x1, Pallas kernels, forward_attention(): pl.pallas_call(functools.partial(forward_kernel, nz), in_specs=[pl.BlockS...  93 us
    pallas_call x1, Pallas kernels, dense(): pl.pallas_call(dense_kernel, grid=(count // tile,), in_specs=[pl.BlockSpe...  39.3 us
    pallas_call x1, Pallas kernels, deliver(): pl.pallas_call(functools.partial(deliver_kernel, mats), grid=(1,), in_spe...  5.82 us

profile of v1, /device:TPU:0, one launch (start us, length us, event | category | flops | bytes accessed | tf_op | source)
XLA Modules:
  0.0 254.5 jit_solution(5335017531609559767)
XLA Ops:
  0.7 0.9 concatenate.5
  1.6 0.6 reshape.102.bias_shard
  2.2 93.0 %shard_map.313 = (bf16[2,2,4,2,96,576]{5,4,3,2,1,0:T(8,128)(2,1)}, bf16[2,2,4,2,24,768]{5,4,3,2,1,0:T(8,128)(2,1)}, bf16[2,2,4,2,96,768]{5,4,3,2,1,0:T(8,128)(2,...) custom-call(s32[2,2]{1,0:T(2,128)} %lengths.5, ...), custom_call_target="tpu_custom_call" | custom-call | tf_op jit(solution)/shard_map/pallas_call | solution.py:968
  95.2 39.3 %shard_map.314 = (bf16[1024,768]{1,0:T(8,128)(2,1)}, bf16[1024,768]{1,0:T(8,128)(2,1)}, bf16[1024,3072]{1,0:T(8,128)(2,1)}, bf16[1024,768]{1,0:T(8,128)(2,1)}, b...) custom-call(s32[2,2]{1,0:T(2,128)} %lengths.5, ...), custom_call_target="tpu_custom_call" | custom-call | flops 22599999488 | bytes 40000000 | tf_op jit(solution)/shard_map/pallas_call | solution.py:1154
  134.4 114.0 %shard_map.315 = (f32[96,768]{1,0:T(8,128)}, f32[96,768]{1,0:T(8,128)}, f32[24,768]{1,0:T(8,128)}, f32[96,192]{1,0:T(8,128)}, f32[96,192]{1,0:T(8,128)}, /*index...) custom-call(s32[2,2]{1,0:T(2,128)} %lengths.5, ...), custom_call_target="tpu_custom_call" | custom-call | tf_op jit(solution)/shard_map/pallas_call | solution.py:1606
  248.5 5.8 %shard_map.316 = (bf16[2,512,768]{2,1,0:T(8,128)(2,1)}, f32[2,512,768]{2,1,0:T(8,128)}, f32[96,768]{1,0:T(8,128)}, f32[96,768]{1,0:T(8,128)}, f32[24,768]{1,0:T(...) custom-call(f32[96,768]{1,0:T(8,128)} %get-tuple-element.95.refs_0_,, ...), custom_call_target="tpu_custom_call" | custom-call | tf_op jit(solution)/shard_map/pallas_call | solution.py:1793
  (2 shorter events, 0.0 us)

commit v2 on v1

--- a/solution.py
+++ b/solution.py
@@ -1180,6 +1180,7 @@
     )(lengths, heads, rows, cots, out_w, up_w, down_w, biases)
 
 
+GRAIN = 64
 BIG = 4
 
 
@@ -1209,16 +1210,15 @@
     vectors_out,
     tokens_out,
     normed_out,
+    joined_kept,
     *refs,
 ):
     parts, heard1, heard2, heard3, heard4 = (refs[BIG * i : BIG * (i + 1)] for i in range(5))
     (
         dense_total,
-        head_total,
+        bias_sums,
         dense_kept,
-        head_kept,
         dense_heard,
-        head_heard,
         acc,
         slots,
         right,
@@ -1251,6 +1251,7 @@
     rows, width = tokens.shape
     half_rows = rows // 2
     chunk, span = 256, 384
+    bias_share = GC // (2 * nz)
     mp, x, c, z, y = positions()
     first, second, partner, along = neighbours(nz)
     own, got1, got2, got3 = regions(x, c, y)
@@ -1288,8 +1289,16 @@
         s = lax.rem(r, 2)
         return pltpu.make_async_copy(heads_grad.at[:, columns(r, PAD)], grad_in.at[s], grad_sem.at[s])
 
-    def w_load(r):
-        return load(w_joined.at[index_of(r)], w_in, 3)
+    w_other = right.at[pl.ds(0, width)]
+
+    def w_load(r, other=False):
+        return load(w_joined.at[index_of(r)], w_other if other else w_in, 6 if other else 3)
+
+    def keep_joined(r):
+        return load(joined, joined_kept.at[r], 5)
+
+    def back_load(r):
+        return slot_load(joined_kept.at[r], lax.rem(r, 2))
 
     ffn_load, attn_low_load = load(ffn_low, right, 0), load(attn_low, right, 0)
     first_load, rows_load = load(first_low, joined, 1), load(rows_in, joined, 1)
@@ -1348,27 +1357,24 @@
         else:
             for k, result in enumerate((query_out, key_out, value_out)):
                 result[...] = total[:, k * GC : (k + 1) * GC]
-
-    kept, heard_sums = (dense_kept, head_kept), (dense_heard, head_heard)
-
-    def sums_copy(v, k):
+            vectors_out[7:9, :bias_share] = total[0:2, 3 * GC : 3 * GC + bias_share]
+
+    def sums_copy(k):
         device = (first, second)[k - 1] if 0 < k < 3 else along[k - 3] if k else partner
-        return remote_copy(
-            kept[v].at[min(k, 3)], heard_sums[v].at[k], v_send.at[v, k], v_recv.at[v, k], device
-        )
-
-    def sums_step(v, k):
-        sums_copy(v, k).wait_recv()
-        kept[v][k + 1] = kept[v][k] + heard_sums[v][k]
+        return remote_copy(dense_kept.at[min(k, 3)], dense_heard.at[k], v_send.at[k], v_recv.at[k], device)
+
+    def sums_step(k):
+        sums_copy(k).wait_recv()
+        dense_kept[k + 1] = dense_kept[k] + dense_heard[k]
         for later in (k + 1,) if k < 2 else range(3, nz + 2):
-            sums_copy(v, later).start()
-
-    def sums_last(v):
-        total = kept[v][3]
+            sums_copy(later).start()
+
+    def sums_last():
+        total = dense_kept[3]
         for k in range(3, nz + 2):
-            sums_copy(v, k).wait_recv()
-            total = total + heard_sums[v][k]
-        (dense_total, head_total)[v][...] = total
+            sums_copy(k).wait_recv()
+            total = total + dense_heard[k]
+        dense_total[...] = total
 
     def finish(p, r):
         gx, gc = group_of(r)
@@ -1382,6 +1388,16 @@
                     if more is not None:
                         value = value + more[i, :, :, at : at + size].astype(jnp.float32)
                     parts[p][gx, gc, i, :, :, at : at + size] = value.astype(low)
+            if p < BIG - 1:
+                return
+            beside = slice(3 * GC, 3 * GC + bias_share)
+            for i in range(nz):
+                for j in range(2):
+                    at = (2 * i + j) * bias_share
+                    value = bias_sums[:, at : at + bias_share]
+                    if more is not None:
+                        value = value + more[i, j, :16, beside].astype(jnp.float32)
+                    parts[p][gx, gc, i, j, :16, beside] = value.astype(low)
 
         @pl.when(r < 2)
         def _():
@@ -1406,9 +1422,13 @@
     active_load(0).start()
     heads_load(0).start()
     first_load.start()
-    w_load(0).start()
+    w_load(3).start()
     tokens_load.start()
     dense_kept[0] = dense_sums[...]
+    bias_sums[...] = jnp.zeros_like(bias_sums)
+    for gx in range(2):
+        for gc in range(2):
+            parts[3][gx, gc, :, :, :, 3 * GC :] = jnp.zeros((nz, 2, width // (2 * nz), GRAIN), low)
     meet([first, second, partner, *along])
     normed_swap = remote_copy(
         normed.at[pl.ds(half_rows, half_rows)], normed_out, swap_sem.at[2], swap_sem.at[3], partner
@@ -1427,7 +1447,7 @@
         return carry
 
     lax.fori_loop(0, GROUPS, down_step, 0)
-    sums_copy(0, 0).start()
+    sums_copy(0).start()
     attn_low_load.start()
     first_load.wait()
     left_t[...] = joined[...].T
@@ -1444,7 +1464,7 @@
         return carry
 
     lax.fori_loop(0, GROUPS, up_step, 0)
-    sums_step(0, 0)
+    sums_step(0)
     attn_low_load.wait()
 
     def out_step(r, carry):
@@ -1456,19 +1476,20 @@
 
     lax.fori_loop(0, GROUPS, out_step, 0)
     grad_load(0).start()
+    w_load(0, True).start()
     rows_load.wait()
     left_t[...] = joined[...].T
     tokens_load.wait()
 
     hooks = {
-        0: lambda: sums_step(0, 1),
+        0: lambda: sums_step(1),
         1: lambda: (pass_first(0), take_second(0, 0)),
-        2: lambda: sums_step(0, 2),
+        2: lambda: sums_step(2),
         4: lambda: take_first(0),
         5: lambda: (pass_first(1), take_second(1, 0)),
         6: lambda: (pass_first(2), take_second(2, 0)),
         8: lambda: take_first(1),
-        9: lambda: (take_first(2), sums_last(0)),
+        9: lambda: (take_first(2), sums_last()),
         10: lambda: take_z(0),
         11: lambda: pl.when(c == 1)(lambda: pass_first(3)),
     }
@@ -1488,6 +1509,7 @@
             for copy in (qkv_load, heads_load, grad_load):
                 copy(r + 1).start()
 
+        pl.when(r == 3)(lambda: back_load(0).start())
         crossed[...] = (grad_in[s].astype(jnp.float32) * heads_in[s].astype(jnp.float32)).T
         keys_t[...] = slots[s, :, PAD : 2 * PAD].T
         key_acc[...] = jnp.zeros_like(key_acc)
@@ -1519,23 +1541,42 @@
 
         lax.fori_loop(0, GH, head_step, 0)
         query_grad = turned[...].T * score_scale
+        pl.when(r > 0)(lambda: keep_joined(r - 1).wait())
         joined[:, :PAD] = query_grad.astype(low)
         joined[:, PAD : 2 * PAD] = (key_acc[...] * score_scale).astype(low)
         joined[:, 2 * PAD :] = value_acc[...].astype(low)
-        head_kept[0, pl.ds(group, 1), :] = jnp.sum(query_grad, axis=0, keepdims=True)
-        head_kept[0, pl.ds(group + GROUPS, 1), :] = jnp.sum(value_acc[...], axis=0, keepdims=True)
+        bias_sums[0:1, :] = jnp.sum(query_grad, axis=0, keepdims=True)
+        bias_sums[1:2, :] = jnp.sum(value_acc[...], axis=0, keepdims=True)
         for at in range(0, width, span):
             acc[at : at + span, :] = product(left_t[at : at + span, :], joined[...])
         finish(3, r)
-        w_load(r).wait()
+        pl.when(r < 3)(lambda: keep_joined(r).start())
+        return carry
+
+    lax.fori_loop(0, GROUPS, group_step, 0)
+    pl.when(c == 0)(lambda: pass_first(3))
+
+    def add_tokens(kept_group, weights):
         for at in range(0, rows, chunk):
-            tokens[at : at + chunk, :] += contract_cols(joined[at : at + chunk, :], w_in[...])
-        pl.when(r < 3)(lambda: w_load(r + 1).start())
-        return carry
-
-    lax.fori_loop(0, GROUPS, group_step, 0)
-    sums_copy(1, 0).start()
-    pl.when(c == 0)(lambda: pass_first(3))
+            tokens[at : at + chunk, :] += contract_cols(kept_group[at : at + chunk, :], weights[...])
+
+    back_load(1).start()
+    w_load(3).wait()
+    add_tokens(joined, w_in)
+    w_load(1).start()
+    w_load(0, True).wait()
+    back_load(0).wait()
+    add_tokens(slots.at[0], w_other)
+    w_load(2, True).start()
+    back_load(2).start()
+    take_second(3, 0)
+    w_load(1).wait()
+    back_load(1).wait()
+    add_tokens(slots.at[1], w_in)
+    take_first(3)
+    w_load(2, True).wait()
+    back_load(2).wait()
+    add_tokens(slots.at[0], w_other)
     swap = remote_copy(
         tokens.at[pl.ds(half_rows, half_rows)], tokens_out.at[c], swap_sem.at[0], swap_sem.at[1], partner
     )
@@ -1558,18 +1599,10 @@
     for k in range(3):
         square = jnp.sum(dense_total[6 + k : 7 + k, :], axis=1, keepdims=True)
         vectors_out[12:13, k : k + 1] = jnp.sqrt(square / (dense_total[9:10, 0:1] * width))
-    sums_step(1, 0)
-    take_second(3, 0)
-    sums_step(1, 1)
     take_z(1)
-    take_first(3)
-    sums_step(1, 2)
     take_z(2)
     take_z(3)
-    sums_last(1)
-
-    vectors_out[7:8, :share] = piece(head_total[pl.ds(mp, 1), :GC], dp, 2 * nz)
-    vectors_out[8:9, :share] = piece(head_total[pl.ds(mp + GROUPS, 1), :GC], dp, 2 * nz)
+
     keep.wait()
     swap.wait()
     normed_swap.wait()
@@ -1580,9 +1613,8 @@
         first_copy(p).wait_send()
         for d in range(nz - 1):
             z_copy(p, d).wait_send()
-    for v in range(2):
-        for k in range(nz + 2):
-            sums_copy(v, k).wait_send()
+    for k in range(nz + 2):
+        sums_copy(k).wait_send()
 
 
 def todo_of(todo):
@@ -1598,19 +1630,20 @@
     rows, width = rows_in.shape
     low, wide = jnp.bfloat16, jnp.float32
     deep = width // (2 * nz)
-    tails = [(deep, width), (deep, width), (GC // (2 * nz), width), (deep, 3 * GC)]
+    tails = [(deep, width), (deep, width), (GC // (2 * nz), width), (deep, 3 * GC + GRAIN)]
     results = [*tails[:3], *[(deep, GC)] * 3]
-    sums = [dense_sums.shape, (2 * GROUPS, PAD)]
+    sums = dense_sums.shape
     anywhere, vmem = pl.BlockSpec(memory_space=pl.ANY), pl.BlockSpec(memory_space=pltpu.VMEM)
     dma = pltpu.SemaphoreType.DMA
     return pl.pallas_call(
         functools.partial(backward_kernel, nz),
         in_specs=[pl.BlockSpec(memory_space=pltpu.SMEM), vmem, vmem, *[anywhere] * len(operands)],
-        out_specs=[*[vmem] * 7, anywhere, anywhere],
+        out_specs=[*[vmem] * 7, *[anywhere] * 3],
         out_shape=[
             *[jax.ShapeDtypeStruct(shape, wide) for shape in (*results, (16, 128))],
             jax.ShapeDtypeStruct((MB, rows // 2, width), wide),
             jax.ShapeDtypeStruct((rows // 2, width), low),
+            jax.ShapeDtypeStruct((GROUPS, rows, 3 * PAD), low),
         ],
         scratch_shapes=[
             *[pltpu.VMEM((2, 2, nz, 2, *t), low) for t in tails],
@@ -1618,9 +1651,10 @@
             *[pltpu.VMEM((2, nz, *t), low) for t in tails],
             *[pltpu.VMEM((nz, *t), low) for t in tails],
             *[pltpu.VMEM((nz - 1, *t), low) for t in tails],
-            *[pltpu.VMEM(shape, wide) for shape in sums],
-            *[pltpu.VMEM((4, *shape), wide) for shape in sums],
-            *[pltpu.VMEM((nz + 2, *shape), wide) for shape in sums],
+            pltpu.VMEM(sums, wide),
+            pltpu.VMEM((16, PAD), wide),
+            pltpu.VMEM((4, *sums), wide),
+            pltpu.VMEM((nz + 2, *sums), wide),
             pltpu.VMEM((width, 3 * PAD), wide),
             pltpu.VMEM((2, rows, width), low),
             pltpu.VMEM((rows, width), low),
@@ -1641,10 +1675,10 @@
             dma((BIG, 5)),
             dma((BIG, nz - 1)),
             dma((BIG, nz - 1)),
-            dma((2, nz + 2)),
-            dma((2, nz + 2)),
+            dma((nz + 2,)),
+            dma((nz + 2,)),
             dma((4,)),
-            dma((5,)),
+            dma((7,)),
             dma((2,)),
             dma((2,)),
             dma((2,)),
@@ -1714,7 +1748,7 @@
         heads_grad,
         dense_sums,
     ) = dense(lengths, heads, rows_in, rows_cot, full_out, full_up, full_down, full_bias)
-    *matrix_grads, vectors, tokens_grad, output_got = backward(
+    *matrix_grads, vectors, tokens_grad, output_got, _ = backward(
         lengths,
         lse,
         dense_sums,

time: 255 us -> 251 us (0.984)
  Pallas kernels: 252 us -> 246 us
    pallas_call x1, Pallas kernels: 114 us -> 108 us  [backward(): pl.pallas_call(functools.partial(backward_kernel, nz), in_specs=[pl.Block...]
where the time goes in v2:
time: 251 us; the launch traced here: 249 us
  Pallas kernels  246 us (98%)
    pallas_call x1, Pallas kernels, backward(): pl.pallas_call(functools.partial(backward_kernel, nz), in_specs=[pl.Block...  108 us
    pallas_call x1, Pallas kernels, forward_attention(): pl.pallas_call(functools.partial(forward_kernel, nz), in_specs=[pl.BlockS...  93 us
    pallas_call x1, Pallas kernels, dense(): pl.pallas_call(dense_kernel, grid=(count // tile,), in_specs=[pl.BlockSpe...  39.3 us
    pallas_call x1, Pallas kernels, deliver(): pl.pallas_call(functools.partial(deliver_kernel, mats), grid=(1,), in_spe...  5.82 us

profile of v2, /device:TPU:0, one launch (start us, length us, event | category | flops | bytes accessed | tf_op | source)
XLA Modules:
  0.0 248.7 jit_solution(7107913426742274874)
XLA Ops:
  0.7 0.9 concatenate.5
  1.6 0.6 reshape.102.bias_shard
  2.2 93.0 %shard_map.313 = (bf16[2,2,4,2,96,576]{5,4,3,2,1,0:T(8,128)(2,1)}, bf16[2,2,4,2,24,768]{5,4,3,2,1,0:T(8,128)(2,1)}, bf16[2,2,4,2,96,768]{5,4,3,2,1,0:T(8,128)(2,...) custom-call(s32[2,2]{1,0:T(2,128)} %lengths.5, ...), custom_call_target="tpu_custom_call" | custom-call | tf_op jit(solution)/shard_map/pallas_call | solution.py:968
  95.2 39.3 %shard_map.314 = (bf16[1024,768]{1,0:T(8,128)(2,1)}, bf16[1024,768]{1,0:T(8,128)(2,1)}, bf16[1024,3072]{1,0:T(8,128)(2,1)}, bf16[1024,768]{1,0:T(8,128)(2,1)}, b...) custom-call(s32[2,2]{1,0:T(2,128)} %lengths.5, ...), custom_call_target="tpu_custom_call" | custom-call | flops 22599999488 | bytes 40000000 | tf_op jit(solution)/shard_map/pallas_call | solution.py:1154
  134.4 108.3 %shard_map.315 = (f32[96,768]{1,0:T(8,128)}, f32[96,768]{1,0:T(8,128)}, f32[24,768]{1,0:T(8,128)}, f32[96,192]{1,0:T(8,128)}, f32[96,192]{1,0:T(8,128)}, /*index...) custom-call(s32[2,2]{1,0:T(2,128)} %lengths.5, ...), custom_call_target="tpu_custom_call" | custom-call | tf_op jit(solution)/shard_map/pallas_call | solution.py:1638
  242.7 5.8 %shard_map.316 = (bf16[2,512,768]{2,1,0:T(8,128)(2,1)}, f32[2,512,768]{2,1,0:T(8,128)}, f32[96,768]{1,0:T(8,128)}, f32[96,768]{1,0:T(8,128)}, f32[24,768]{1,0:T(...) custom-call(f32[96,768]{1,0:T(8,128)} %get-tuple-element.95.refs_0_,, ...), custom_call_target="tpu_custom_call" | custom-call | tf_op jit(solution)/shard_map/pallas_call | solution.py:1827
  (2 shorter events, 0.0 us)

commit v3 on v2

--- a/solution.py
+++ b/solution.py
@@ -1482,16 +1482,15 @@
     tokens_load.wait()
 
     hooks = {
-        0: lambda: sums_step(1),
         1: lambda: (pass_first(0), take_second(0, 0)),
-        2: lambda: sums_step(2),
+        2: lambda: sums_step(1),
         4: lambda: take_first(0),
-        5: lambda: (pass_first(1), take_second(1, 0)),
-        6: lambda: (pass_first(2), take_second(2, 0)),
-        8: lambda: take_first(1),
-        9: lambda: (take_first(2), sums_last()),
-        10: lambda: take_z(0),
-        11: lambda: pl.when(c == 1)(lambda: pass_first(3)),
+        6: lambda: (pass_first(1), take_second(1, 0)),
+        7: lambda: (pass_first(2), take_second(2, 0)),
+        8: lambda: sums_step(2),
+        9: lambda: take_first(1),
+        10: lambda: take_first(2),
+        11: lambda: (take_z(0), sums_last(), pl.when(c == 1)(lambda: pass_first(3))),
     }
     row = lax.broadcasted_iota(jnp.int32, (rows, 1), 0)
     bias = jnp.where(place_of(c, row, half_rows) < lengths[c, x], 0.0, masked_score).astype(low)

time: 251 us -> 237 us (0.944)
  Pallas kernels: 246 us -> 234 us
    pallas_call x1, Pallas kernels: 108 us -> 95.8 us  [backward(): pl.pallas_call(functools.partial(backward_kernel, nz), in_specs=[pl.Block...]
where the time goes in v3:
time: 237 us; the launch traced here: 236 us
  Pallas kernels  234 us (99%)
    pallas_call x1, Pallas kernels, backward(): pl.pallas_call(functools.partial(backward_kernel, nz), in_specs=[pl.Block...  95.8 us
    pallas_call x1, Pallas kernels, forward_attention(): pl.pallas_call(functools.partial(forward_kernel, nz), in_specs=[pl.BlockS...  93 us
    pallas_call x1, Pallas kernels, dense(): pl.pallas_call(dense_kernel, grid=(count // tile,), in_specs=[pl.BlockSpe...  39.3 us
    pallas_call x1, Pallas kernels, deliver(): pl.pallas_call(functools.partial(deliver_kernel, mats), grid=(1,), in_spe...  5.82 us

profile of v3, /device:TPU:0, one launch (start us, length us, event | category | flops | bytes accessed | tf_op | source)
XLA Modules:
  0.0 236.2 jit_solution(16880746439024397864)
XLA Ops:
  0.7 0.9 concatenate.5
  1.6 0.6 reshape.102.bias_shard
  2.2 93.0 %shard_map.313 = (bf16[2,2,4,2,96,576]{5,4,3,2,1,0:T(8,128)(2,1)}, bf16[2,2,4,2,24,768]{5,4,3,2,1,0:T(8,128)(2,1)}, bf16[2,2,4,2,96,768]{5,4,3,2,1,0:T(8,128)(2,...) custom-call(s32[2,2]{1,0:T(2,128)} %lengths.5, ...), custom_call_target="tpu_custom_call" | custom-call | tf_op jit(solution)/shard_map/pallas_call | solution.py:968
  95.2 39.3 %shard_map.314 = (bf16[1024,768]{1,0:T(8,128)(2,1)}, bf16[1024,768]{1,0:T(8,128)(2,1)}, bf16[1024,3072]{1,0:T(8,128)(2,1)}, bf16[1024,768]{1,0:T(8,128)(2,1)}, b...) custom-call(s32[2,2]{1,0:T(2,128)} %lengths.5, ...), custom_call_target="tpu_custom_call" | custom-call | flops 22599999488 | bytes 40000000 | tf_op jit(solution)/shard_map/pallas_call | solution.py:1154
  134.4 95.8 %shard_map.315 = (f32[96,768]{1,0:T(8,128)}, f32[96,768]{1,0:T(8,128)}, f32[24,768]{1,0:T(8,128)}, f32[96,192]{1,0:T(8,128)}, f32[96,192]{1,0:T(8,128)}, /*index...) custom-call(s32[2,2]{1,0:T(2,128)} %lengths.5, ...), custom_call_target="tpu_custom_call" | custom-call | tf_op jit(solution)/shard_map/pallas_call | solution.py:1637
  230.2 5.8 %shard_map.316 = (bf16[2,512,768]{2,1,0:T(8,128)(2,1)}, f32[2,512,768]{2,1,0:T(8,128)}, f32[96,768]{1,0:T(8,128)}, f32[96,768]{1,0:T(8,128)}, f32[24,768]{1,0:T(...) custom-call(f32[96,768]{1,0:T(8,128)} %get-tuple-element.95.refs_0_,, ...), custom_call_target="tpu_custom_call" | custom-call | tf_op jit(solution)/shard_map/pallas_call | solution.py:1826
  (2 shorter events, 0.0 us)
